TPU v7x, 512 devices: a whole 4x4x16 slice. The times are simulated.
512 devices in a mesh: gx: 16 (over x, y), gy: 32 (over z, core).
Axes of the slice: x: 4, y: 4, z: 16, core: 2. Of those that a mesh axis runs over, the one named last changes fastest.
Arguments:
- right_side: float32 [128, 256, 256], P('gx', 'gy'), may hold values from -6 to 6
- coefficient: float32 [128, 256, 256], P('gx', 'gy'), may hold values from 0.5 to 4
Outputs:
- solution_field: float32 [128, 256, 256], P('gx', 'gy')
All inputs are finite; a program needn't handle non-finite values.
Results may differ from a plain program's by a relative error of at most 0.000078.
Values sent between devices are 32-bit elements; how exact they have to be, the bound alone decides.
A program may use at most 64 MiB of HBM per device.

v0:
```python
import jax
import jax.numpy as jnp
from jax import lax
from jax.sharding import PartitionSpec as P

LEVELS = 3
SMOOTH = 2
COARSE_STEPS = 6


SMOOTH_LOW = 0.5
SMOOTH_HIGH = 2.0
COARSE_LOW = 0.05
COARSE_HIGH = 2.0


def with_halo(value, sides, width):
    for axis, dim in sides:
        count, length = (lax.axis_size(axis), value.shape[dim])
        up = [(i, (i + 1) % count) for i in range(count - 1)]
        down = [(j, i) for i, j in up]
        last = lax.slice_in_dim(value, length - width, length, axis=dim)
        leading = lax.slice_in_dim(value, 0, width, axis=dim)
        before = lax.ppermute(last, axis, up)
        after = lax.ppermute(leading, axis, down)
        value = jnp.concatenate([before, value, after], axis=dim)
    return value


def chebyshev(low_end, high_end, sweeps):
    middle = 0.5 * (high_end + low_end)
    half_span = 0.5 * (high_end - low_end)
    sig_ratio = middle / half_span
    rho_now = 1.0 / sig_ratio
    coeff_pairs = []
    for sweep_num in range(1, sweeps):
        rho_next = 1.0 / (2.0 * sig_ratio - rho_now)
        coeff_pairs.append((rho_next * rho_now, 2.0 * rho_next / half_span))
        rho_now = rho_next
    return (1.0 / middle, coeff_pairs)


def neighbours(padded):
    return [
        padded[2:, 1:-1, 1:-1],
        padded[:-2, 1:-1, 1:-1],
        padded[1:-1, 2:, 1:-1],
        padded[1:-1, :-2, 1:-1],
        padded[1:-1, 1:-1, 2:],
        padded[1:-1, 1:-1, :-2],
    ]


def face_weights(padded):
    centre = padded[1:-1, 1:-1, 1:-1]
    weights = [0.5 * (centre + beside_cell) for beside_cell in neighbours(padded)]
    diagonal = weights[0] + weights[1] + weights[2] + weights[3] + weights[4] + weights[5]
    return (weights, diagonal)


def apply_operator(padded, weights, diagonal):
    beside_list = neighbours(padded)
    summed = weights[0] * beside_list[0]
    for face_num in range(1, 6):
        summed = summed + weights[face_num] * beside_list[face_num]
    return diagonal * padded[1:-1, 1:-1, 1:-1] - summed


def restrict_sum(field):
    field = field[0::2] + field[1::2]
    field = field[:, 0::2] + field[:, 1::2]
    return field[:, :, 0::2] + field[:, :, 1::2]


def pad_depth(field):
    return jnp.pad(field, ((0, 0), (0, 0), (1, 1)))


def prolong_axis(padded, axis_num):
    length = padded.shape[axis_num] - 2
    centre = lax.slice_in_dim(padded, 1, length + 1, axis=axis_num)
    before = lax.slice_in_dim(padded, 0, length, axis=axis_num)
    following = lax.slice_in_dim(padded, 2, length + 2, axis=axis_num)
    even_part = 0.75 * centre + 0.25 * before
    odd_part = 0.75 * centre + 0.25 * following
    joined = jnp.stack([even_part, odd_part], axis=axis_num + 1)
    new_shape = list(centre.shape)
    new_shape[axis_num] = 2 * length
    return joined.reshape(new_shape)


def depth_weights(coarse_len):
    row_ids = jnp.arange(coarse_len + 2, dtype=jnp.int32)[:, None]
    col_ids = jnp.arange(2 * coarse_len, dtype=jnp.int32)[None, :]
    home_row = col_ids // 2 + 1
    near_row = jnp.where(col_ids % 2 == 0, home_row - 1, home_row + 1)
    return jnp.where(row_ids == home_row, 0.75, 0.0).astype(jnp.float32) + jnp.where(
        row_ids == near_row, 0.25, 0.0
    ).astype(jnp.float32)


def prolong_local(padded):
    padded = prolong_axis(padded, 0)
    padded = prolong_axis(padded, 1)
    coarse_len = padded.shape[2] - 2
    flattened = padded.reshape(-1, coarse_len + 2)
    fine_vals = jnp.dot(
        flattened,
        depth_weights(coarse_len),
        precision=lax.Precision.HIGHEST,
        preferred_element_type=jnp.float32,
    )
    return fine_vals.reshape(padded.shape[0], padded.shape[1], 2 * coarse_len)


def residual_each(iterate, source, weights, diagonal):
    padded = pad_depth(with_halo(iterate, (("gx", 0), ("gy", 1)), 1))
    return source - apply_operator(padded, weights, diagonal)


def smooth_each(iterate, source, weights, diagonal, inverse):
    inv_mid, coeff_pairs = chebyshev(SMOOTH_LOW, SMOOTH_HIGH, SMOOTH)
    residue = source if iterate is None else residual_each(iterate, source, weights, diagonal)
    step_dir = residue * inverse * inv_mid
    iterate = step_dir if iterate is None else iterate + step_dir
    for keep_part, push_part in coeff_pairs:
        residue = residual_each(iterate, source, weights, diagonal)
        step_dir = keep_part * step_dir + push_part * (residue * inverse)
        iterate = iterate + step_dir
    return iterate


def smooth_whole(source, coeffs):
    weights, diagonal = face_weights(jnp.pad(coeffs, 1))
    inverse = 1.0 / diagonal
    inv_mid, coeff_pairs = chebyshev(COARSE_LOW, COARSE_HIGH, COARSE_STEPS)
    step_dir = source * inverse * inv_mid
    iterate = step_dir
    for keep_part, push_part in coeff_pairs:
        residue = source - apply_operator(jnp.pad(iterate, 1), weights, diagonal)
        step_dir = keep_part * step_dir + push_part * (residue * inverse)
        iterate = iterate + step_dir
    residue = source - apply_operator(jnp.pad(iterate, 1), weights, diagonal)
    ones_image = apply_operator(jnp.pad(jnp.ones_like(source), 1), weights, diagonal)
    return iterate + jnp.sum(residue) / jnp.sum(ones_image)


def assemble(pieces, brick_rows, brick_cols, brick_depth):
    along_x = lax.axis_size("gx")
    along_y = lax.axis_size("gy")
    blocks = pieces.reshape(along_x, along_y, brick_rows, brick_cols, brick_depth)
    return blocks.transpose(0, 2, 1, 3, 4).reshape(
        along_x * brick_rows, along_y * brick_cols, brick_depth
    )


def coarse_solve(source, coeffs):
    brick_rows, brick_cols, brick_depth = source.shape
    pieces = (
        lax.all_gather(source[None], ("gx", "gy"), axis=0, tiled=True),
        lax.all_gather(coeffs[None], ("gx", "gy"), axis=0, tiled=True),
    )
    whole_source = assemble(pieces[0], brick_rows, brick_cols, brick_depth)
    whole_coeffs = assemble(pieces[1], brick_rows, brick_cols, brick_depth)
    iterate = smooth_whole(whole_source, whole_coeffs)
    return lax.dynamic_slice(
        iterate,
        (lax.axis_index("gx") * brick_rows, lax.axis_index("gy") * brick_cols, 0),
        (brick_rows, brick_cols, brick_depth),
    )


def body(right_side, coefficient):
    source = right_side
    coeffs = coefficient
    stored = []
    for level_num in range(LEVELS - 1):
        coeff_pad = pad_depth(with_halo(coeffs, (("gx", 0), ("gy", 1)), 1))
        weights, diagonal = face_weights(coeff_pad)
        inverse = 1.0 / diagonal
        iterate = smooth_each(None, source, weights, diagonal, inverse)
        extended = None
        residue = residual_each(iterate, source, weights, diagonal)
        stored.append((iterate, source, weights, diagonal, inverse, extended))
        source = 0.5 * restrict_sum(residue)
        coeffs = 0.125 * restrict_sum(coeffs)
    coarse = coarse_solve(source, coeffs)
    for iterate, source, weights, diagonal, inverse, extended in reversed(stored):
        padded = pad_depth(with_halo(coarse, (("gx", 0), ("gy", 1)), 1))
        iterate = iterate + prolong_local(padded)
        coarse = smooth_each(iterate, source, weights, diagonal, inverse)
    return coarse


def solution(mesh):
    placed = (P("gx", "gy", None), P("gx", "gy", None))
    return jax.shard_map(
        body, mesh=mesh, in_specs=placed, out_specs=P("gx", "gy", None), check_vma=False
    )
```

profile of v0, /device:TPU:130, one launch (start us, length us, event | category | flops | bytes accessed | tf_op | source)
XLA Modules:
  0.0 502.8 jit_solution(13105966415424009518)
XLA Ops:
  0.8 3.5 collective-permute-start.1
  4.3 4.5 collective-permute-start
  19.5 6.3 %collective-permute-start.4 = (f32[1,8,256]{2,1,0:T(8,128)S(1)}, f32[1,8,256]{2,1,0:T(8,128)S(1)}, u32[]{:S(2)}, u32[]{:S(2)}) collective-permute-start(f32[1,8,256]{2,1,0:T(8,128)S(1)} %get-tuple-element.55), channel_id=1, source_target_pairs={{32,0},{64,32},{96,64},{128,96},{160,128},{192,160},{224,192},{256... | collective-permute-start | bytes 24584 | tf_op jit(solution)/shard_map/ppermute | solution.py:25
  27.8 5.7 %collective-permute-done.5 = f32[1,8,256]{2,1,0:T(8,128)S(1)} collective-permute-done((f32[1,8,256]{2,1,0:T(8,128)S(1)}, f32[1,8,256]{2,1,0:T(8,128)S(1)}, u32[]{:S(2)}, u32[]{:S(2)}) %collective-permute-start.5) | collective-permute-done | bytes 8224 | tf_op jit(solution)/shard_map/ppermute | solution.py:24
  39.8 3.9 collective-permute-start.13
  44.1 4.0 collective-permute-start.8
  50.1 3.8 collective-permute-start.14
  55.9 4.9 collective-permute-start.10
  62.8 4.1 collective-permute-done.11
  68.2 5.8 %collective-permute-start.16 = (f32[1,4,128]{2,1,0:T(4,128)S(1)}, f32[1,4,128]{2,1,0:T(4,128)S(1)}, u32[]{:S(2)}, u32[]{:S(2)}) collective-permute-start(f32[1,4,128]{2,1,0:T(4,128)S(1)} %get-tuple-element.87), channel_id=1, source_target_pairs={{32,0},{64,32},{96,64},{128,96},{160,128},{192,160},{224,192},{256... | collective-permute-start | bytes 6152 | tf_op jit(solution)/shard_map/ppermute | solution.py:25
  75.9 5.6 %collective-permute-done.17 = f32[1,4,128]{2,1,0:T(4,128)S(1)} collective-permute-done((f32[1,4,128]{2,1,0:T(4,128)S(1)}, f32[1,4,128]{2,1,0:T(4,128)S(1)}, u32[]{:S(2)}, u32[]{:S(2)}) %collective-permute-start.17) | collective-permute-done | bytes 2080 | tf_op jit(solution)/shard_map/ppermute | solution.py:24
  91.7 3.9 collective-permute-start.21
  95.7 3.6 collective-permute-done.21
  103.6 133.0 %all-gather.1 = f32[1024,2,64]{2,1,0:T(2,128)S(1)} all-gather(f32[2,2,64]{2,1,0:T(2,128)S(1)} %add_multiply_fusion.2), channel_id=3, replica_groups=mesh['gx'=16,'gy'=32] {'gx','gy'}, dimensions={0}, use_global_device_ids=true | all-gather | bytes 525312 | tf_op jit(solution)/shard_map/all_gather | solution.py:161
  237.7 130.7 %all-gather = f32[1024,2,64]{2,1,0:T(2,128)S(1)} all-gather(f32[2,2,64]{2,1,0:T(2,128)S(1)} %add_multiply_fusion.3), channel_id=2, replica_groups=mesh['gx'=16,'gy'=32] {'gx','gy'}, dimensions={0}, use_global_device_ids=true | all-gather | bytes 525312 | tf_op jit(solution)/shard_map/all_gather | solution.py:160
  385.2 5.8 %collective-permute-start.25 = (f32[1,2,64]{2,1,0:T(2,128)S(1)}, f32[1,2,64]{2,1,0:T(2,128)S(1)}, u32[]{:S(2)}, u32[]{:S(2)}) collective-permute-start(f32[1,2,64]{2,1,0:T(2,128)S(1)} %get-tuple-element.93), channel_id=1, source_target_pairs={{32,0},{64,32},{96,64},{128,96},{160,128},{192,160},{224,192},{256... | collective-permute-start | bytes 1544 | tf_op jit(solution)/shard_map/ppermute | solution.py:25
  394.3 4.9 collective-permute-start.27
  400.8 6.3 %collective-permute-start.28 = (f32[1,4,128]{2,1,0:T(4,128)S(1)}, f32[1,4,128]{2,1,0:T(4,128)S(1)}, u32[]{:S(2)}, u32[]{:S(2)}) collective-permute-start(f32[1,4,128]{2,1,0:T(4,128)S(1)} %get-tuple-element.79), channel_id=1, source_target_pairs={{32,0},{64,32},{96,64},{128,96},{160,128},{192,160},{224,192},{256... | collective-permute-start | bytes 6152 | tf_op jit(solution)/shard_map/ppermute | solution.py:25
  409.0 5.6 %collective-permute-done.29 = f32[1,4,128]{2,1,0:T(4,128)S(1)} collective-permute-done((f32[1,4,128]{2,1,0:T(4,128)S(1)}, f32[1,4,128]{2,1,0:T(4,128)S(1)}, u32[]{:S(2)}, u32[]{:S(2)}) %collective-permute-start.29) | collective-permute-done | bytes 2080 | tf_op jit(solution)/shard_map/ppermute | solution.py:24
  420.0 4.2 collective-permute-done.31
  426.3 3.9 collective-permute-start.33
  430.2 3.7 collective-permute-done.33
  438.3 3.7 collective-permute-done.35
  444.1 6.0 %collective-permute-start.37 = (f32[1,4,128]{2,1,0:T(4,128)S(1)}, f32[1,4,128]{2,1,0:T(4,128)S(1)}, u32[]{:S(2)}, u32[]{:S(2)}) collective-permute-start(f32[1,4,128]{2,1,0:T(4,128)S(1)} %get-tuple-element.75), channel_id=1, source_target_pairs={{32,0},{64,32},{96,64},{128,96},{160,128},{192,160},{224,192},{256... | collective-permute-start | bytes 6152 | tf_op jit(solution)/shard_map/ppermute | solution.py:25
  453.4 4.9 collective-permute-start.39
  460.2 6.3 %collective-permute-start.40 = (f32[1,8,256]{2,1,0:T(8,128)S(1)}, f32[1,8,256]{2,1,0:T(8,128)S(1)}, u32[]{:S(2)}, u32[]{:S(2)}) collective-permute-start(f32[1,8,256]{2,1,0:T(8,128)S(1)} %get-tuple-element.51), channel_id=1, source_target_pairs={{32,0},{64,32},{96,64},{128,96},{160,128},{192,160},{224,192},{256... | collective-permute-start | bytes 24584 | tf_op jit(solution)/shard_map/ppermute | solution.py:25
  468.4 5.7 %collective-permute-done.41 = f32[1,8,256]{2,1,0:T(8,128)S(1)} collective-permute-done((f32[1,8,256]{2,1,0:T(8,128)S(1)}, f32[1,8,256]{2,1,0:T(8,128)S(1)}, u32[]{:S(2)}, u32[]{:S(2)}) %collective-permute-start.41) | collective-permute-done | bytes 8224 | tf_op jit(solution)/shard_map/ppermute | solution.py:24
  474.2 3.4 collective-permute-start.42
  479.5 4.3 collective-permute-done.43
  486.0 3.9 collective-permute-start.45
  490.0 3.7 collective-permute-done.45
  498.1 3.8 collective-permute-done.47
  (176 shorter events, 97.0 us)
Async XLA Ops:
  0.8 8.0 %collective-permute-start.1 = (f32[1,8,256]{2,1,0:T(8,128)S(1)}, f32[1,8,256]{2,1,0:T(8,128)S(1)}, u32[]{:S(2)}, u32[]{:S(2)}) collective-permute-start(f32[1,8,256]{2,1,0:T(8,128)S(1)} %get-tuple-element.56), channel_id=1, source_target_pairs={{0,32},{32,64},{64,96},{96,128},{128,160},{160,192},{192,224},{224... | collective-permute-start | bytes 24584 | tf_op jit(solution)/shard_map/ppermute | solution.py:24
  12.0 6.2 %collective-permute-start.3 = (f32[10,1,256]{2,1,0:T(1,128)S(1)}, f32[10,1,256]{2,1,0:T(1,128)S(1)}, u32[]{:S(2)}, u32[]{:S(2)}) collective-permute-start(f32[10,1,256]{2,1,0:T(1,128)S(1)} %get-tuple-element.46), channel_id=1, source_target_pairs={{0,1},{1,2},{2,3},{3,4},{4,5},{5,6},{6,7},{7,8},{8,9},{9,10},{10,1... | collective-permute-start | bytes 30728 | tf_op jit(solution)/shard_map/ppermute | solution.py:24
  19.5 8.3 %collective-permute-start.4 = (f32[1,8,256]{2,1,0:T(8,128)S(1)}, f32[1,8,256]{2,1,0:T(8,128)S(1)}, u32[]{:S(2)}, u32[]{:S(2)}) collective-permute-start(f32[1,8,256]{2,1,0:T(8,128)S(1)} %get-tuple-element.55), channel_id=1, source_target_pairs={{32,0},{64,32},{96,64},{128,96},{160,128},{192,160},{224,192},{256... | collective-permute-start | bytes 24584 | tf_op jit(solution)/shard_map/ppermute | solution.py:25
  25.8 7.7 %collective-permute-start.5 = (f32[1,8,256]{2,1,0:T(8,128)S(1)}, f32[1,8,256]{2,1,0:T(8,128)S(1)}, u32[]{:S(2)}, u32[]{:S(2)}) collective-permute-start(f32[1,8,256]{2,1,0:T(8,128)S(1)} %get-tuple-element.54), channel_id=1, source_target_pairs={{0,32},{32,64},{64,96},{96,128},{128,160},{160,192},{192,224},{224... | collective-permute-start | bytes 24584 | tf_op jit(solution)/shard_map/ppermute | solution.py:24
  33.5 10.2 %collective-permute-start.6 = (f32[10,1,256]{2,1,0:T(1,128)S(1)}, f32[10,1,256]{2,1,0:T(1,128)S(1)}, u32[]{:S(2)}, u32[]{:S(2)}) collective-permute-start(f32[10,1,256]{2,1,0:T(1,128)S(1)} %get-tuple-element.45), channel_id=1, source_target_pairs={{1,0},{2,1},{3,2},{4,3},{5,4},{6,5},{7,6},{8,7},{9,8},{10,9},{11,1... | collective-permute-start | bytes 30728 | tf_op jit(solution)/shard_map/ppermute | solution.py:25
  35.4 8.3 %collective-permute-start.7 = (f32[10,1,256]{2,1,0:T(1,128)S(1)}, f32[10,1,256]{2,1,0:T(1,128)S(1)}, u32[]{:S(2)}, u32[]{:S(2)}) collective-permute-start(f32[10,1,256]{2,1,0:T(1,128)S(1)} %get-tuple-element.44), channel_id=1, source_target_pairs={{0,1},{1,2},{2,3},{3,4},{4,5},{5,6},{6,7},{7,8},{8,9},{9,10},{10,1... | collective-permute-start | bytes 30728 | tf_op jit(solution)/shard_map/ppermute | solution.py:24
  37.9 12.2 %collective-permute-start.12 = (f32[1,4,128]{2,1,0:T(4,128)S(1)}, f32[1,4,128]{2,1,0:T(4,128)S(1)}, u32[]{:S(2)}, u32[]{:S(2)}) collective-permute-start(f32[1,4,128]{2,1,0:T(4,128)S(1)} %get-tuple-element.88), channel_id=1, source_target_pairs={{32,0},{64,32},{96,64},{128,96},{160,128},{192,160},{224,192},{256... | collective-permute-start | bytes 6152 | tf_op jit(solution)/shard_map/ppermute | solution.py:25
  39.8 10.3 %collective-permute-start.13 = (f32[1,4,128]{2,1,0:T(4,128)S(1)}, f32[1,4,128]{2,1,0:T(4,128)S(1)}, u32[]{:S(2)}, u32[]{:S(2)}) collective-permute-start(f32[1,4,128]{2,1,0:T(4,128)S(1)} %get-tuple-element.89), channel_id=1, source_target_pairs={{0,32},{32,64},{64,96},{96,128},{128,160},{160,192},{192,224},{224... | collective-permute-start | bytes 6152 | tf_op jit(solution)/shard_map/ppermute | solution.py:24
  44.1 11.8 %collective-permute-start.8 = (f32[1,8,256]{2,1,0:T(8,128)S(1)}, f32[1,8,256]{2,1,0:T(8,128)S(1)}, u32[]{:S(2)}, u32[]{:S(2)}) collective-permute-start(f32[1,8,256]{2,1,0:T(8,128)S(1)} %get-tuple-element.53), channel_id=1, source_target_pairs={{32,0},{64,32},{96,64},{128,96},{160,128},{192,160},{224,192},{256... | collective-permute-start | bytes 24584 | tf_op jit(solution)/shard_map/ppermute | solution.py:25
  48.1 7.7 %collective-permute-start.9 = (f32[1,8,256]{2,1,0:T(8,128)S(1)}, f32[1,8,256]{2,1,0:T(8,128)S(1)}, u32[]{:S(2)}, u32[]{:S(2)}) collective-permute-start(f32[1,8,256]{2,1,0:T(8,128)S(1)} %get-tuple-element.52), channel_id=1, source_target_pairs={{0,32},{32,64},{64,96},{96,128},{128,160},{160,192},{192,224},{224... | collective-permute-start | bytes 24584 | tf_op jit(solution)/shard_map/ppermute | solution.py:24
  50.1 12.6 %collective-permute-start.14 = (f32[6,1,128]{2,1,0:T(1,128)S(1)}, f32[6,1,128]{2,1,0:T(1,128)S(1)}, u32[]{:S(2)}, u32[]{:S(2)}) collective-permute-start(f32[6,1,128]{2,1,0:T(1,128)S(1)} %get-tuple-element.73), channel_id=1, source_target_pairs={{1,0},{2,1},{3,2},{4,3},{5,4},{6,5},{7,6},{8,7},{9,8},{10,9},{11,1... | collective-permute-start | bytes 9224 | tf_op jit(solution)/shard_map/ppermute | solution.py:25
  53.9 8.8 %collective-permute-start.15 = (f32[6,1,128]{2,1,0:T(1,128)S(1)}, f32[6,1,128]{2,1,0:T(1,128)S(1)}, u32[]{:S(2)}, u32[]{:S(2)}) collective-permute-start(f32[6,1,128]{2,1,0:T(1,128)S(1)} %get-tuple-element.72), channel_id=1, source_target_pairs={{0,1},{1,2},{2,3},{3,4},{4,5},{5,6},{6,7},{7,8},{8,9},{9,10},{10,1... | collective-permute-start | bytes 9224 | tf_op jit(solution)/shard_map/ppermute | solution.py:24
  55.9 6.9 %collective-permute-start.10 = (f32[10,1,256]{2,1,0:T(1,128)S(1)}, f32[10,1,256]{2,1,0:T(1,128)S(1)}, u32[]{:S(2)}, u32[]{:S(2)}) collective-permute-start(f32[10,1,256]{2,1,0:T(1,128)S(1)} %get-tuple-element.43), channel_id=1, source_target_pairs={{1,0},{2,1},{3,2},{4,3},{5,4},{6,5},{7,6},{8,7},{9,8},{10,9},{11,1... | collective-permute-start | bytes 30728 | tf_op jit(solution)/shard_map/ppermute | solution.py:25
  68.2 7.7 %collective-permute-start.16 = (f32[1,4,128]{2,1,0:T(4,128)S(1)}, f32[1,4,128]{2,1,0:T(4,128)S(1)}, u32[]{:S(2)}, u32[]{:S(2)}) collective-permute-start(f32[1,4,128]{2,1,0:T(4,128)S(1)} %get-tuple-element.87), channel_id=1, source_target_pairs={{32,0},{64,32},{96,64},{128,96},{160,128},{192,160},{224,192},{256... | collective-permute-start | bytes 6152 | tf_op jit(solution)/shard_map/ppermute | solution.py:25
  73.9 7.6 %collective-permute-start.17 = (f32[1,4,128]{2,1,0:T(4,128)S(1)}, f32[1,4,128]{2,1,0:T(4,128)S(1)}, u32[]{:S(2)}, u32[]{:S(2)}) collective-permute-start(f32[1,4,128]{2,1,0:T(4,128)S(1)} %get-tuple-element.86), channel_id=1, source_target_pairs={{0,32},{32,64},{64,96},{96,128},{128,160},{160,192},{192,224},{224... | collective-permute-start | bytes 6152 | tf_op jit(solution)/shard_map/ppermute | solution.py:24
  91.7 7.6 %collective-permute-start.21 = (f32[1,4,128]{2,1,0:T(4,128)S(1)}, f32[1,4,128]{2,1,0:T(4,128)S(1)}, u32[]{:S(2)}, u32[]{:S(2)}) collective-permute-start(f32[1,4,128]{2,1,0:T(4,128)S(1)} %get-tuple-element.84), channel_id=1, source_target_pairs={{0,32},{32,64},{64,96},{96,128},{128,160},{160,192},{192,224},{224... | collective-permute-start | bytes 6152 | tf_op jit(solution)/shard_map/ppermute | solution.py:24
  99.3 137.8 %collective-permute-start.22 = (f32[6,1,128]{2,1,0:T(1,128)S(1)}, f32[6,1,128]{2,1,0:T(1,128)S(1)}, u32[]{:S(2)}, u32[]{:S(2)}) collective-permute-start(f32[6,1,128]{2,1,0:T(1,128)S(1)} %get-tuple-element.69), channel_id=1, source_target_pairs={{1,0},{2,1},{3,2},{4,3},{5,4},{6,5},{7,6},{8,7},{9,8},{10,9},{11,1... | collective-permute-start | bytes 9224 | tf_op jit(solution)/shard_map/ppermute | solution.py:25
  101.2 135.9 %collective-permute-start.23 = (f32[6,1,128]{2,1,0:T(1,128)S(1)}, f32[6,1,128]{2,1,0:T(1,128)S(1)}, u32[]{:S(2)}, u32[]{:S(2)}) collective-permute-start(f32[6,1,128]{2,1,0:T(1,128)S(1)} %get-tuple-element.68), channel_id=1, source_target_pairs={{0,1},{1,2},{2,3},{3,4},{4,5},{5,6},{6,7},{7,8},{8,9},{9,10},{10,1... | collective-permute-start | bytes 9224 | tf_op jit(solution)/shard_map/ppermute | solution.py:24
  383.1 8.0 %collective-permute-start.24 = (f32[1,2,64]{2,1,0:T(2,128)S(1)}, f32[1,2,64]{2,1,0:T(2,128)S(1)}, u32[]{:S(2)}, u32[]{:S(2)}) collective-permute-start(f32[1,2,64]{2,1,0:T(2,128)S(1)} %get-tuple-element.92), channel_id=1, source_target_pairs={{0,32},{32,64},{64,96},{96,128},{128,160},{160,192},{192,224},{224... | collective-permute-start | bytes 1544 | tf_op jit(solution)/shard_map/ppermute | solution.py:24
  385.2 7.1 %collective-permute-start.25 = (f32[1,2,64]{2,1,0:T(2,128)S(1)}, f32[1,2,64]{2,1,0:T(2,128)S(1)}, u32[]{:S(2)}, u32[]{:S(2)}) collective-permute-start(f32[1,2,64]{2,1,0:T(2,128)S(1)} %get-tuple-element.93), channel_id=1, source_target_pairs={{32,0},{64,32},{96,64},{128,96},{160,128},{192,160},{224,192},{256... | collective-permute-start | bytes 1544 | tf_op jit(solution)/shard_map/ppermute | solution.py:25
  392.3 6.8 %collective-permute-start.26 = (f32[4,1,64]{2,1,0:T(1,128)S(1)}, f32[4,1,64]{2,1,0:T(1,128)S(1)}, u32[]{:S(2)}, u32[]{:S(2)}) collective-permute-start(f32[4,1,64]{2,1,0:T(1,128)S(1)} %get-tuple-element.90), channel_id=1, source_target_pairs={{0,1},{1,2},{2,3},{3,4},{4,5},{5,6},{6,7},{7,8},{8,9},{9,10},{10,1... | collective-permute-start | bytes 3080 | tf_op jit(solution)/shard_map/ppermute | solution.py:24
  400.8 8.2 %collective-permute-start.28 = (f32[1,4,128]{2,1,0:T(4,128)S(1)}, f32[1,4,128]{2,1,0:T(4,128)S(1)}, u32[]{:S(2)}, u32[]{:S(2)}) collective-permute-start(f32[1,4,128]{2,1,0:T(4,128)S(1)} %get-tuple-element.79), channel_id=1, source_target_pairs={{32,0},{64,32},{96,64},{128,96},{160,128},{192,160},{224,192},{256... | collective-permute-start | bytes 6152 | tf_op jit(solution)/shard_map/ppermute | solution.py:25
  407.1 7.6 %collective-permute-start.29 = (f32[1,4,128]{2,1,0:T(4,128)S(1)}, f32[1,4,128]{2,1,0:T(4,128)S(1)}, u32[]{:S(2)}, u32[]{:S(2)}) collective-permute-start(f32[1,4,128]{2,1,0:T(4,128)S(1)} %get-tuple-element.78), channel_id=1, source_target_pairs={{0,32},{32,64},{64,96},{96,128},{128,160},{160,192},{192,224},{224... | collective-permute-start | bytes 6152 | tf_op jit(solution)/shard_map/ppermute | solution.py:24
  426.3 7.6 %collective-permute-start.33 = (f32[1,4,128]{2,1,0:T(4,128)S(1)}, f32[1,4,128]{2,1,0:T(4,128)S(1)}, u32[]{:S(2)}, u32[]{:S(2)}) collective-permute-start(f32[1,4,128]{2,1,0:T(4,128)S(1)} %get-tuple-element.76), channel_id=1, source_target_pairs={{0,32},{32,64},{64,96},{96,128},{128,160},{160,192},{192,224},{224... | collective-permute-start | bytes 6152 | tf_op jit(solution)/shard_map/ppermute | solution.py:24
  442.2 8.0 %collective-permute-start.36 = (f32[1,4,128]{2,1,0:T(4,128)S(1)}, f32[1,4,128]{2,1,0:T(4,128)S(1)}, u32[]{:S(2)}, u32[]{:S(2)}) collective-permute-start(f32[1,4,128]{2,1,0:T(4,128)S(1)} %get-tuple-element.74), channel_id=1, source_target_pairs={{0,32},{32,64},{64,96},{96,128},{128,160},{160,192},{192,224},{224... | collective-permute-start | bytes 6152 | tf_op jit(solution)/shard_map/ppermute | solution.py:24
  444.1 7.3 %collective-permute-start.37 = (f32[1,4,128]{2,1,0:T(4,128)S(1)}, f32[1,4,128]{2,1,0:T(4,128)S(1)}, u32[]{:S(2)}, u32[]{:S(2)}) collective-permute-start(f32[1,4,128]{2,1,0:T(4,128)S(1)} %get-tuple-element.75), channel_id=1, source_target_pairs={{32,0},{64,32},{96,64},{128,96},{160,128},{192,160},{224,192},{256... | collective-permute-start | bytes 6152 | tf_op jit(solution)/shard_map/ppermute | solution.py:25
  451.5 6.8 %collective-permute-start.38 = (f32[6,1,128]{2,1,0:T(1,128)S(1)}, f32[6,1,128]{2,1,0:T(1,128)S(1)}, u32[]{:S(2)}, u32[]{:S(2)}) collective-permute-start(f32[6,1,128]{2,1,0:T(1,128)S(1)} %get-tuple-element.62), channel_id=1, source_target_pairs={{0,1},{1,2},{2,3},{3,4},{4,5},{5,6},{6,7},{7,8},{8,9},{9,10},{10,1... | collective-permute-start | bytes 9224 | tf_op jit(solution)/shard_map/ppermute | solution.py:24
  460.2 8.2 %collective-permute-start.40 = (f32[1,8,256]{2,1,0:T(8,128)S(1)}, f32[1,8,256]{2,1,0:T(8,128)S(1)}, u32[]{:S(2)}, u32[]{:S(2)}) collective-permute-start(f32[1,8,256]{2,1,0:T(8,128)S(1)} %get-tuple-element.51), channel_id=1, source_target_pairs={{32,0},{64,32},{96,64},{128,96},{160,128},{192,160},{224,192},{256... | collective-permute-start | bytes 24584 | tf_op jit(solution)/shard_map/ppermute | solution.py:25
  466.5 7.7 %collective-permute-start.41 = (f32[1,8,256]{2,1,0:T(8,128)S(1)}, f32[1,8,256]{2,1,0:T(8,128)S(1)}, u32[]{:S(2)}, u32[]{:S(2)}) collective-permute-start(f32[1,8,256]{2,1,0:T(8,128)S(1)} %get-tuple-element.50), channel_id=1, source_target_pairs={{0,32},{32,64},{64,96},{96,128},{128,160},{160,192},{192,224},{224... | collective-permute-start | bytes 24584 | tf_op jit(solution)/shard_map/ppermute | solution.py:24
  477.6 6.2 %collective-permute-start.43 = (f32[10,1,256]{2,1,0:T(1,128)S(1)}, f32[10,1,256]{2,1,0:T(1,128)S(1)}, u32[]{:S(2)}, u32[]{:S(2)}) collective-permute-start(f32[10,1,256]{2,1,0:T(1,128)S(1)} %get-tuple-element.40), channel_id=1, source_target_pairs={{0,1},{1,2},{2,3},{3,4},{4,5},{5,6},{6,7},{7,8},{8,9},{9,10},{10,1... | collective-permute-start | bytes 30728 | tf_op jit(solution)/shard_map/ppermute | solution.py:24
  486.0 7.7 %collective-permute-start.45 = (f32[1,8,256]{2,1,0:T(8,128)S(1)}, f32[1,8,256]{2,1,0:T(8,128)S(1)}, u32[]{:S(2)}, u32[]{:S(2)}) collective-permute-start(f32[1,8,256]{2,1,0:T(8,128)S(1)} %get-tuple-element.48), channel_id=1, source_target_pairs={{0,32},{32,64},{64,96},{96,128},{128,160},{160,192},{192,224},{224... | collective-permute-start | bytes 24584 | tf_op jit(solution)/shard_map/ppermute | solution.py:24
  495.6 6.2 %collective-permute-start.47 = (f32[10,1,256]{2,1,0:T(1,128)S(1)}, f32[10,1,256]{2,1,0:T(1,128)S(1)}, u32[]{:S(2)}, u32[]{:S(2)}) collective-permute-start(f32[10,1,256]{2,1,0:T(1,128)S(1)} %get-tuple-element.38), channel_id=1, source_target_pairs={{0,1},{1,2},{2,3},{3,4},{4,5},{5,6},{6,7},{7,8},{8,9},{9,10},{10,1... | collective-permute-start | bytes 30728 | tf_op jit(solution)/shard_map/ppermute | solution.py:24
  (18 other events, 178.2 us)
where the time goes:
time: 504 us; the launch traced here: 503 us
  blocking collectives  264 us (52%)
  starting transfers between devices  148 us (29%)
  waiting for transfers between devices  65 us (13%)
  other arithmetic  18 us (4%)
  local copies, waits for them, and re-layouts  5.18 us (1%)
    all_gather x1, blocking collectives, coarse_solve(): lax.all_gather(coeffs[None], ('gx', 'gy'), axis=0, tiled=True)  133 us
    all_gather x1, blocking collectives, coarse_solve(): lax.all_gather(source[None], ('gx', 'gy'), axis=0, tiled=True)  131 us
    ppermute x24, starting transfers between devices, with_halo(): after = lax.ppermute(leading, axis, down)  89.4 us
    ppermute x24, waiting for transfers between devices, with_halo(): before = lax.ppermute(last, axis, up)  59.4 us
    ppermute x24, starting transfers between devices, with_halo(): before = lax.ppermute(last, axis, up)  58.7 us
  transfers between devices with their start and end apart: 48, of which 19 were waited for; matrix products, arithmetic and copies ran while one was open for 1% of the time, Pallas kernels for 0%

commit v1 on v0

v1 whole, which is shorter than its diff:
```python
import jax
import jax.numpy as jnp
from jax import lax
from jax.experimental import pallas as pl
from jax.experimental.pallas import tpu as pltpu
from jax.sharding import PartitionSpec as P

SMOOTH_LOW = 0.5
SMOOTH_HIGH = 2.0
COARSE_LOW = 0.05
COARSE_HIGH = 2.0
COARSE_STEPS = 6

F32 = jnp.float32
NXD, NYD = 16, 32
NX, NY, NZ = 128, 256, 256
R5 = 5
R4 = 4
MESH = pl.DeviceIdType.MESH
NEAR = [(a, b) for a in (-1, 0, 1) for b in (-1, 0, 1) if (a, b) != (0, 0)]


def chebyshev(low_end, high_end, sweeps):
    middle = 0.5 * (high_end + low_end)
    half_span = 0.5 * (high_end - low_end)
    sig_ratio = middle / half_span
    rho_now = 1.0 / sig_ratio
    pairs = []
    for _ in range(1, sweeps):
        rho_next = 1.0 / (2.0 * sig_ratio - rho_now)
        pairs.append((rho_next * rho_now, 2.0 * rho_next / half_span))
        rho_now = rho_next
    return 1.0 / middle, pairs


def iota(shape, dim):
    return lax.broadcasted_iota(jnp.int32, shape, dim)


def dot(a, b):
    return jnp.dot(a, b, precision=lax.Precision.HIGHEST, preferred_element_type=F32)


def up1(v):
    return pltpu.roll(v, v.shape[0] - 1, 0)


def dn1(v):
    return pltpu.roll(v, 1, 0)


def lup(v):
    return pltpu.roll(v, v.shape[1] - 1, 1)


def ldn(v):
    return pltpu.roll(v, 1, 1)


def interp(out_cell, in_cell):
    home = out_cell >> 1
    near = jnp.where((out_cell & 1) == 0, home - 1, home + 1)
    return jnp.where(in_cell == home, 0.75, 0.0).astype(F32) + jnp.where(in_cell == near, 0.25, 0.0).astype(F32)


def pair_sum(fine, coarse):
    r, c = iota((fine, coarse), 0), iota((fine, coarse), 1)
    return jnp.where((r >> 1) == c, 1.0, 0.0).astype(F32)


class Level:
    def __init__(self, refs, planes, rows, lanes, zfull):
        self.c, self.wx, self.wy, self.wz, self.dg, self.iv = refs
        self.planes, self.rows, self.lanes, self.zfull = planes, rows, lanes, zfull

    def build(self, mask_of, lo, hi):
        lane = iota((self.rows, self.lanes), 1)
        c = self.c[lo - 1]
        for i in range(lo - 1, hi):
            nxt = self.c[i + 1]
            wxp = 0.5 * (c + nxt)
            self.wx[i] = wxp
            if i >= lo:
                wyp = 0.5 * (c + up1(c))
                wym = dn1(wyp)
                if self.zfull:
                    wzp = 0.5 * (c + jnp.where(lane == self.lanes - 1, 0.0, lup(c)))
                    wzm = 0.5 * (c + jnp.where(lane == 0, 0.0, ldn(c)))
                    wz = jnp.where(lane == self.lanes - 1, 0.0, wzp)
                else:
                    wzp = 0.5 * (c + lup(c))
                    wzm = ldn(wzp)
                    wz = wzp
                diag = wxp + self.wx[i - 1] + wyp + wym + wzp + wzm
                m = mask_of(i)
                self.wy[i] = wyp
                self.wz[i] = wz
                self.dg[i] = diag
                self.iv[i] = m / jnp.where(m > 0.5, diag, 1.0)
            c = nxt

    def apply(self, v, i):
        x = v[i]
        s = self.wx[i] * v[i + 1] + self.wx[i - 1] * v[i - 1]
        wy = self.wy[i]
        s = s + wy * up1(x) + dn1(wy * x)
        wz = self.wz[i]
        s = s + wz * lup(x) + ldn(wz * x)
        return self.dg[i] * x - s


def body_kernel(f_ref, c_ref, o_ref,
                sy, rxf, rxc, ry, rcf, rcc, f0, v0a, v0b, l0,
                sc1, rc1, sf1, rf1, su1, ru1, f1, u1, v1a, v1b, l1,
                sc2, gc2, ac2, sf2, gf2, af2, f2, v2a, v2b, d2, l2,
                r0b, r1b, lp1, lp0, rz0, rz1, pz1, pz0,
                sg1, rg1, sg2, rg2, ssem, rsem, gsem):
    mx, my = lax.axis_index("gx"), lax.axis_index("gy")

    def dev(a, b):
        return (lax.rem(mx + (a + NXD), NXD), lax.rem(my + (b + NYD), NYD))

    partners = [(a, b) for a, b in NEAR if a and b]
    partners += [(0, b) for b in range(1, NYD)] + [(a, 0) for a in range(1, NXD)]
    barrier = pltpu.get_barrier_semaphore()
    for a, b in partners:
        pl.semaphore_signal(barrier, inc=1, device_id=dev(a, b), device_id_type=MESH)

    sends = []

    def send(src, dst, a, b):
        k = len(sends)
        copy = pltpu.make_async_remote_copy(src_ref=src, dst_ref=dst, send_sem=ssem.at[k], recv_sem=rsem.at[k],
                                            device_id=dev(a, b), device_id_type=MESH)
        copy.start()
        sends.append(copy)
        return copy

    for p in range(8):
        fp, cp = f_ref[p], c_ref[p]
        for s in (0, 1):
            sy[s, 0, p] = fp[4 * s : 4 * s + 4]
            sy[s, 1, p] = cp[4 * s : 4 * s + 4]
    rz0[...] = pair_sum(256, 128)
    rz1[...] = pair_sum(128, 128)
    o, q = iota((16, 64), 0), iota((16, 64), 1)
    lc1 = jnp.where(((q >> 4) == (o >> 2)) & (((q & 7) >> 1) == (o & 3)), 0.125, 0.0).astype(F32)
    c1own = dot(dot(lc1, c_ref[...].reshape(64, 256)), rz0[...])
    sc1[...] = c1own.reshape(4, 4, 128)
    o, q = iota((4, 16), 0), iota((4, 16), 1)
    lc2 = jnp.where(((q >> 3) == (o >> 1)) & (((q & 3) >> 1) == (o & 1)), 0.125, 0.0).astype(F32)
    sc2[...] = dot(dot(lc2, c1own), rz1[...])
    zed = jnp.zeros((16, 256), F32)
    for p in (0, 1, 2, 3, 12, 13, 14, 15):
        f0[p] = zed
        l0[0][p] = zed
    pl.semaphore_wait(barrier, len(partners))

    wait_a = []
    for s, a in ((1, 1), (0, -1)):
        wait_a.append(send(c_ref.at[4:8] if s else c_ref.at[0:4], rxc.at[1 - s], a, 0))
        wait_a.append(send(f_ref.at[5:8] if s else f_ref.at[0:3], rxf.at[1 - s], a, 0))
    for sx, a in ((1, 1), (0, -1)):
        for s, b in ((1, 1), (0, -1)):
            wait_a.append(send(sy.at[s, 1, 5:8] if sx else sy.at[s, 1, 0:3], rcc.at[1 - sx, 1 - s], a, b))
            wait_a.append(send(sy.at[s, 0, 6:8] if sx else sy.at[s, 0, 0:2], rcf.at[1 - sx, 1 - s], a, b))
    for s, b in ((1, 1), (0, -1)):
        wait_a.append(send(sy.at[s], ry.at[1 - s], 0, b))
    offs5 = [k for k in range(-R5, R5 + 1) if k]
    offs4 = [k for k in range(-R4, R4 + 1) if k]
    wait_c2 = [send(sc2, gc2.at[R5 - k], 0, k) for k in offs5]
    wait_c1 = [send(sc1, rc1.at[n], a, b) for n, (a, b) in enumerate(NEAR)]

    o, q = iota((16, 128), 0), iota((16, 128), 1)
    yr = (q & 15) - 4
    lr0 = jnp.where(((q >> 5) == (o >> 2)) & ((yr >> 1) == (o & 3)) & (yr >= 0) & (yr < 8), 0.5, 0.0).astype(F32)
    o, q = iota((4, 64), 0), iota((4, 64), 1)
    yr = (q & 15) - 4
    lr1 = jnp.where(((q >> 5) == (o >> 1)) & ((yr >> 1) == (o & 1)) & (yr >= 0) & (yr < 4), 0.5, 0.0).astype(F32)

    def prolong_matrix(planes_out, x_out0, x_in0, rows_in, planes_in, y_out0, y_in0, bx, by, nx, ny):
        shape = (planes_out * 16, planes_in * rows_in)
        r, c = iota(shape, 0), iota(shape, 1)
        xo, yo = (r >> 4) + x_out0, (r & 15) + y_out0
        if rows_in == 16:
            ci, cr = c >> 4, c & 15
        else:
            ci = (c * 2731) >> 16
            cr = c - ci * rows_in
        w = interp(xo, ci + x_in0) * interp(yo, cr + y_in0)
        gx_, gy_ = xo + mx * bx, yo + my * by
        ok = (gx_ >= 0) & (gx_ < nx) & (gy_ >= 0) & (gy_ < ny)
        return jnp.where(ok, w, 0.0)

    lp1[...] = prolong_matrix(12, -4, -3, 24, 8, -4, -10, 4, 4, 64, 128)
    lp0[...] = prolong_matrix(12, -2, -2, 16, 8, -4, -4, 8, 8, 128, 256)
    r, c = iota((128, 128), 0), iota((128, 128), 1)
    pz1[...] = jnp.where(r < 64, interp(c, r), 0.0)
    r, c = iota((128, 256), 0), iota((128, 256), 1)
    pz0[...] = interp(c, r)

    def masker(rows, lanes, halo, b, nx, ny, valid_lanes, valid_rows):
        row = iota((rows, lanes), 0)
        y = row - halo + my * b
        ok = (y >= 0) & (y < ny) & (row < valid_rows)
        if valid_lanes < lanes:
            ok = ok & (iota((rows, lanes), 1) < valid_lanes)
        base = jnp.where(ok, 1.0, 0.0).astype(F32)

        def mask_of(i):
            x = mx * b + (i - halo)
            return base * jnp.where((x >= 0) & (x < nx), 1.0, 0.0).astype(F32)

        return mask_of

    mask0 = masker(16, 256, 4, 8, NX, NY, 256, 16)
    mask1 = masker(16, 128, 4, 4, NX // 2, NY // 2, 128, 12)
    mask2 = masker(24, 128, 10, 2, NX // 4, NY // 4, 64, 22)

    def spread2(mine, got, rows, cells, offs):
        rows[0, 20:24] = jnp.zeros((4, 128), F32)
        rows[1, 20:24] = jnp.zeros((4, 128), F32)
        for k in [0] + offs:
            g = mine[...] if k == 0 else got[k + R5]
            for x in (0, 1):
                rows[x, 2 * (k + R5) : 2 * (k + R5) + 2] = g[2 * x : 2 * x + 2]
        cells[10] = rows[0]
        cells[11] = rows[1]

    for w in wait_c2:
        w.wait_recv()
    spread2(sc2, gc2, ac2, l2[0], offs5)
    wait_c2 = [send(ac2, l2[0].at[2 * (R5 - k) : 2 * (R5 - k) + 2], k, 0) for k in offs5]

    for w in wait_a:
        w.wait_recv()
    c0 = l0[0]
    for p in range(8):
        i = p + 4
        f0[i, 0:4] = ry[0, 0, p]
        f0[i, 4:12] = f_ref[p]
        f0[i, 12:16] = ry[1, 0, p]
        c0[i, 0:4] = ry[0, 1, p]
        c0[i, 4:12] = c_ref[p]
        c0[i, 12:16] = ry[1, 1, p]
    for p in range(4):
        c0[p, 4:12] = rxc[0, p]
        c0[12 + p, 4:12] = rxc[1, p]
    for p in range(3):
        f0[1 + p, 4:12] = rxf[0, p]
        f0[12 + p, 4:12] = rxf[1, p]
        for s in (0, 1):
            c0[1 + p, 12 * s : 12 * s + 4] = rcc[0, s, p]
            c0[12 + p, 12 * s : 12 * s + 4] = rcc[1, s, p]
    for p in range(2):
        for s in (0, 1):
            f0[2 + p, 12 * s : 12 * s + 4] = rcf[0, s, p]
            f0[12 + p, 12 * s : 12 * s + 4] = rcf[1, s, p]
    for i in range(16):
        c0[i] = c0[i] * mask0(i)
    lev0 = Level(l0, 16, 16, 256, True)
    lev0.build(mask0, 1, 15)

    inv_mid, ((keep, push),) = chebyshev(SMOOTH_LOW, SMOOTH_HIGH, 2)

    def first(lev, f, v, lo, hi):
        for i in range(lo, hi):
            v[i] = f[i] * lev.iv[i] * inv_mid

    def second(lev, f, va, vb, lo, hi):
        for i in range(lo, hi):
            d = va[i]
            r = f[i] - lev.apply(va, i)
            vb[i] = d + (keep * d + push * (r * lev.iv[i]))

    def residual(lev, f, v, out, lo, hi):
        for i in range(lo, hi):
            out[i - lo] = f[i] - lev.apply(v, i)

    v0a[0] = zed
    v0a[15] = zed
    first(lev0, f0, v0a, 1, 15)
    second(lev0, f0, v0a, v0b, 2, 14)
    residual(lev0, f0, v0b, r0b, 4, 12)
    f1own = dot(dot(lr0, r0b[...].reshape(128, 256)), rz0[...])
    sf1[...] = f1own.reshape(4, 4, 128)
    wait_f1 = [send(sf1, rf1.at[n], a, b) for n, (a, b) in enumerate(NEAR)]

    def spread1(mine, got, cells):
        for n, (a, b) in enumerate([(0, 0)] + NEAR):
            for p in range(4):
                x, y = 4 - 4 * a + p, 4 - 4 * b
                cells[x, y : y + 4] = mine[p] if n == 0 else got[n - 1, p]

    zed1 = jnp.zeros((4, 128), F32)
    for i in range(12):
        l1[0][i, 12:16] = zed1
        f1[i, 12:16] = zed1
        u1[i, 12:16] = zed1
    for w in wait_c1:
        w.wait_recv()
    spread1(sc1, rc1, l1[0])
    for i in range(12):
        l1[0][i] = l1[0][i] * mask1(i)
    lev1 = Level(l1, 12, 16, 128, True)
    lev1.build(mask1, 1, 11)
    for w in wait_c2:
        w.wait_recv()
    for i in range(22):
        l2[0][i] = l2[0][i] * mask2(i)
    lev2 = Level(l2, 22, 24, 128, False)
    lev2.build(mask2, 2, 20)

    for w in wait_f1:
        w.wait_recv()
    spread1(sf1, rf1, f1)
    first(lev1, f1, v1a, 1, 11)
    second(lev1, f1, v1a, v1b, 2, 10)
    for p in range(4):
        su1[p] = v1b[4 + p, 4:8]
    residual(lev1, f1, v1b, r1b, 4, 8)
    sf2[...] = dot(dot(lr1, r1b[...].reshape(64, 128)), rz1[...])
    wait_f2 = [send(sf2, gf2.at[R5 - k], 0, k) for k in offs4]
    wait_u1 = [send(su1, ru1.at[n], a, b) for n, (a, b) in enumerate(NEAR)]

    for x in (0, 1):
        af2[x, 0:2] = jnp.zeros((2, 128), F32)
        af2[x, 20:24] = jnp.zeros((4, 128), F32)
    for w in wait_f2:
        w.wait_recv()
    for k in [0] + offs4:
        g = sf2[...] if k == 0 else gf2[k + R5]
        for x in (0, 1):
            af2[x, 2 * (k + R5) : 2 * (k + R5) + 2] = g[2 * x : 2 * x + 2]
    f2[10] = af2[0]
    f2[11] = af2[1]
    wait_f2 = [send(af2, f2.at[2 * (R5 - k) : 2 * (R5 - k) + 2], k, 0) for k in offs4]

    for w in wait_u1:
        w.wait_recv()
    spread1(su1, ru1, u1)
    for i in range(12):
        u1[i] = u1[i] * mask1(i)

    for w in wait_f2:
        w.wait_recv()
    mid2, pairs2 = chebyshev(COARSE_LOW, COARSE_HIGH, COARSE_STEPS)
    for i in range(2, 20):
        d = f2[i] * lev2.iv[i] * mid2
        v2a[i] = d
        d2[i] = d
    va, vb = v2a, v2b
    for m, (k2, p2) in enumerate(pairs2):
        for i in range(3 + m, 19 - m):
            r = f2[i] - lev2.apply(va, i)
            d = k2 * d2[i] + p2 * (r * lev2.iv[i])
            d2[i] = d
            vb[i] = va[i] + d
        va, vb = vb, va

    num = jnp.zeros((24, 128), F32)
    den = jnp.zeros((24, 128), F32)
    row = iota((24, 128), 0)
    own = jnp.where((row == 10) | (row == 11), mask2(10), 0.0)
    for i in range(9, 13):
        vb[i] = mask2(i)
    for i in (10, 11):
        num = num + own * (f2[i] - lev2.apply(va, i))
        den = den + own * lev2.apply(vb, i)
    sg1[0:1] = jnp.sum(num, axis=0, keepdims=True)
    sg1[1:2] = jnp.sum(den, axis=0, keepdims=True)

    def broadcast(mine, got, count, offset_of, k):
        copies = []
        for n in range(1, count):
            copy = pltpu.make_async_remote_copy(src_ref=mine, dst_ref=got.at[n - 1], send_sem=gsem.at[2 * k], recv_sem=gsem.at[2 * k + 1],
                                                device_id=dev(*offset_of(n)), device_id_type=MESH)
            copy.start()
        whole = pltpu.make_async_remote_copy(src_ref=got, dst_ref=got, send_sem=gsem.at[2 * k], recv_sem=gsem.at[2 * k + 1],
                                             device_id=dev(*offset_of(1)), device_id_type=MESH)
        whole.wait_recv()
        whole.wait_send()
        return mine[...] + jnp.sum(got[...], axis=0)

    sg2[...] = broadcast(sg1, rg1, NYD, lambda n: (0, n), 0)
    total = broadcast(sg2, rg2, NXD, lambda n: (n, 0), 1)
    num = jnp.sum(total[0:1], axis=1, keepdims=True)
    den = jnp.sum(total[1:2], axis=1, keepdims=True)
    shift = num / den
    for i in range(7, 15):
        va[i] = va[i] + shift * mask2(i)

    def post(lev, f, v, w, lo, hi, out=None):
        for i in range(lo, hi):
            w[i] = v[i] + (f[i] - lev.apply(v, i)) * lev.iv[i] * inv_mid
        for i in range(lo + 1, hi - 1):
            d = w[i] - v[i]
            r = f[i] - lev.apply(w, i)
            e = w[i] + (keep * d + push * (r * lev.iv[i]))
            if out is None:
                v[i] = e
            else:
                out[i - lo - 1] = e[4:12]

    p1 = dot(dot(lp1[...], va[7:15].reshape(192, 128)), pz1[...]).reshape(12, 16, 128)
    for i in range(12):
        u1[i] = u1[i] + p1[i]
    post(lev1, f1, u1, v1a, 1, 11)
    p0 = dot(dot(lp0[...], u1[2:10].reshape(128, 128)), pz0[...]).reshape(12, 16, 256)
    for i in range(12):
        v0b[i + 2] = v0b[i + 2] + p0[i]
    post(lev0, f0, v0b, v0a, 3, 13, o_ref)

    for w in sends:
        w.wait_send()


def solution(mesh):
    def vm(*shape):
        return pltpu.VMEM(shape, F32)

    def level(*shape):
        return [vm(*shape) for _ in range(6)]

    nsend = 4 + 8 + 2 + 10 + 8 + 10 + 8 + 8 + 8 + 8
    scratch = [
        vm(2, 2, 8, 4, 256), vm(2, 3, 8, 256), vm(2, 4, 8, 256), vm(2, 2, 8, 4, 256), vm(2, 2, 2, 4, 256), vm(2, 2, 3, 4, 256),
        vm(16, 16, 256), vm(16, 16, 256), vm(16, 16, 256), level(16, 16, 256),
        vm(4, 4, 128), vm(8, 4, 4, 128), vm(4, 4, 128), vm(8, 4, 4, 128), vm(4, 4, 128), vm(8, 4, 4, 128),
        vm(12, 16, 128), vm(12, 16, 128), vm(12, 16, 128), vm(12, 16, 128), level(12, 16, 128),
        vm(4, 128), vm(11, 4, 128), vm(2, 24, 128), vm(4, 128), vm(11, 4, 128), vm(2, 24, 128),
        vm(22, 24, 128), vm(22, 24, 128), vm(22, 24, 128), vm(22, 24, 128), level(22, 24, 128),
        vm(8, 16, 256), vm(4, 16, 128), vm(192, 192), vm(192, 128), vm(256, 128), vm(128, 128), vm(128, 128), vm(128, 256),
        vm(2, 128), vm(NYD - 1, 2, 128), vm(2, 128), vm(NXD - 1, 2, 128),
        pltpu.SemaphoreType.DMA((nsend,)), pltpu.SemaphoreType.DMA((nsend,)), pltpu.SemaphoreType.DMA((4,)),
    ]

    def body(right_side, coefficient):
        return pl.pallas_call(
            body_kernel,
            out_shape=jax.ShapeDtypeStruct((8, 8, 256), F32),
            in_specs=[pl.BlockSpec(memory_space=pltpu.VMEM)] * 2,
            out_specs=pl.BlockSpec(memory_space=pltpu.VMEM),
            scratch_shapes=scratch,
            compiler_params=pltpu.CompilerParams(collective_id=0, has_side_effects=True),
        )(right_side, coefficient)

    placed = (P("gx", "gy", None), P("gx", "gy", None))
    return jax.shard_map(body, mesh=mesh, in_specs=placed, out_specs=P("gx", "gy", None), check_vma=False)
```

time: 504 us -> 56.9 us (0.11)
  the two profiles are of different devices: /device:TPU:130 before, /device:TPU:1 now
where the time goes in v1:
time: 56.9 us; the launch traced here: 56.7 us
  Pallas kernels  55.3 us (97%)
  local copies, waits for them, and re-layouts  1.47 us (3%)
    pallas_call x1, Pallas kernels, body(): pl.pallas_call(body_kernel, out_shape=jax.ShapeDtypeStruct((8, 8, 256), F...  55.3 us
    unnamed x1, local copies, waits for them, and re-layouts  1.47 us

profile of v1, /device:TPU:1, one launch (start us, length us, event | category | flops | bytes accessed | tf_op | source)
XLA Modules:
  0.0 56.7 jit_solution(374912934928478817)
XLA Ops:
  0.0 55.3 %shard_map.28 = f32[8,8,256]{2,1,0:T(8,128)} custom-call(f32[8,8,256]{2,1,0:T(8,128)} %f_ref.1, f32[8,8,256]{2,1,0:T(8,128)} %c_ref.1), custom_call_target="tpu_custom_call" | custom-call | tf_op jit(solution)/shard_map/pallas_call | solution.py:439
  55.3 1.5 %copy.4 = f32[8,8,256]{2,1,0:T(8,128)} copy(f32[8,8,256]{2,1,0:T(8,128)} %shard_map.28) | data formatting | bytes 131072

commit v2 on v1

--- a/solution.py
+++ b/solution.py
@@ -112,16 +112,16 @@
 def body_kernel(f_ref, c_ref, o_ref,
                 sy, rxf, rxc, ry, rcf, rcc, f0, v0a, v0b, l0,
                 sc1, rc1, sf1, rf1, su1, ru1, f1, u1, v1a, v1b, l1,
-                sc2, gc2, ac2, sf2, gf2, af2, f2, v2a, v2b, d2, l2,
-                r0b, r1b, lp1, lp0, rz0, rz1, pz1, pz0,
-                sg1, rg1, sg2, rg2, ssem, rsem, gsem):
+                sc2, gc2, ac2, rc2, sf2, gf2, af2, rf2, f2, v2a, v2b, d2, l2,
+                r0b, r1b, lp1, lp0, rz0, rz1, pz1, pz0, hw, hx, y1, y0, yout,
+                sg1, rg1, sg2, rg2, ssem, rsem, gsem, far):
     mx, my = lax.axis_index("gx"), lax.axis_index("gy")
 
     def dev(a, b):
         return (lax.rem(mx + (a + NXD), NXD), lax.rem(my + (b + NYD), NYD))
 
     partners = [(a, b) for a, b in NEAR if a and b]
-    partners += [(0, b) for b in range(1, NYD)] + [(a, 0) for a in range(1, NXD)]
+    partners += [(0, b) for b in range(-R5, R5 + 1) if b] + [(a, 0) for a in range(-R5, R5 + 1) if a]
     barrier = pltpu.get_barrier_semaphore()
     for a, b in partners:
         pl.semaphore_signal(barrier, inc=1, device_id=dev(a, b), device_id_type=MESH)
@@ -136,40 +136,44 @@
         sends.append(copy)
         return copy
 
+    def pack2(v):
+        return v[0:2] + pltpu.roll(v[2:4], 64, 1)
+
+    rz0[...] = pair_sum(256, 128)
+    rz1[...] = pair_sum(128, 128)
+    o, q = iota((16, 64), 0), iota((16, 64), 1)
+    lc1 = jnp.where(((q >> 4) == (o >> 2)) & (((q & 7) >> 1) == (o & 3)), 0.125, 0.0).astype(F32)
+    c1own = dot(dot(lc1, c_ref[...].reshape(64, 256)), rz0[...])
+    o, q = iota((4, 16), 0), iota((4, 16), 1)
+    lc2 = jnp.where(((q >> 3) == (o >> 1)) & (((q & 3) >> 1) == (o & 1)), 0.125, 0.0).astype(F32)
+    sc2[...] = pack2(dot(dot(lc2, c1own), rz1[...]))
+    sc1[...] = c1own.reshape(4, 4, 128)
     for p in range(8):
         fp, cp = f_ref[p], c_ref[p]
         for s in (0, 1):
             sy[s, 0, p] = fp[4 * s : 4 * s + 4]
             sy[s, 1, p] = cp[4 * s : 4 * s + 4]
-    rz0[...] = pair_sum(256, 128)
-    rz1[...] = pair_sum(128, 128)
-    o, q = iota((16, 64), 0), iota((16, 64), 1)
-    lc1 = jnp.where(((q >> 4) == (o >> 2)) & (((q & 7) >> 1) == (o & 3)), 0.125, 0.0).astype(F32)
-    c1own = dot(dot(lc1, c_ref[...].reshape(64, 256)), rz0[...])
-    sc1[...] = c1own.reshape(4, 4, 128)
-    o, q = iota((4, 16), 0), iota((4, 16), 1)
-    lc2 = jnp.where(((q >> 3) == (o >> 1)) & (((q & 3) >> 1) == (o & 1)), 0.125, 0.0).astype(F32)
-    sc2[...] = dot(dot(lc2, c1own), rz1[...])
+    pl.semaphore_wait(barrier, len(partners))
+
+    offs5 = [k for k in range(-R5, R5 + 1) if k]
+    offs4 = [k for k in range(-R4, R4 + 1) if k]
+    wait_c2 = [send(sc2, gc2.at[R5 - k], 0, k) for k in offs5]
+    wait_a = []
+    for sx, a in ((1, 1), (0, -1)):
+        for s, b in ((1, 1), (0, -1)):
+            wait_a.append(send(sy.at[s, 1, 5:8] if sx else sy.at[s, 1, 0:3], rcc.at[1 - sx, 1 - s], a, b))
+            wait_a.append(send(sy.at[s, 0, 6:8] if sx else sy.at[s, 0, 0:2], rcf.at[1 - sx, 1 - s], a, b))
+    for s, a in ((1, 1), (0, -1)):
+        wait_a.append(send(c_ref.at[4:8] if s else c_ref.at[0:4], rxc.at[1 - s], a, 0))
+        wait_a.append(send(f_ref.at[5:8] if s else f_ref.at[0:3], rxf.at[1 - s], a, 0))
+    for s, b in ((1, 1), (0, -1)):
+        wait_a.append(send(sy.at[s], ry.at[1 - s], 0, b))
+    wait_c1 = [send(sc1, rc1.at[n], a, b) for n, (a, b) in enumerate(NEAR)]
+
     zed = jnp.zeros((16, 256), F32)
     for p in (0, 1, 2, 3, 12, 13, 14, 15):
         f0[p] = zed
         l0[0][p] = zed
-    pl.semaphore_wait(barrier, len(partners))
-
-    wait_a = []
-    for s, a in ((1, 1), (0, -1)):
-        wait_a.append(send(c_ref.at[4:8] if s else c_ref.at[0:4], rxc.at[1 - s], a, 0))
-        wait_a.append(send(f_ref.at[5:8] if s else f_ref.at[0:3], rxf.at[1 - s], a, 0))
-    for sx, a in ((1, 1), (0, -1)):
-        for s, b in ((1, 1), (0, -1)):
-            wait_a.append(send(sy.at[s, 1, 5:8] if sx else sy.at[s, 1, 0:3], rcc.at[1 - sx, 1 - s], a, b))
-            wait_a.append(send(sy.at[s, 0, 6:8] if sx else sy.at[s, 0, 0:2], rcf.at[1 - sx, 1 - s], a, b))
-    for s, b in ((1, 1), (0, -1)):
-        wait_a.append(send(sy.at[s], ry.at[1 - s], 0, b))
-    offs5 = [k for k in range(-R5, R5 + 1) if k]
-    offs4 = [k for k in range(-R4, R4 + 1) if k]
-    wait_c2 = [send(sc2, gc2.at[R5 - k], 0, k) for k in offs5]
-    wait_c1 = [send(sc1, rc1.at[n], a, b) for n, (a, b) in enumerate(NEAR)]
 
     o, q = iota((16, 128), 0), iota((16, 128), 1)
     yr = (q & 15) - 4
@@ -217,20 +221,25 @@
     mask1 = masker(16, 128, 4, 4, NX // 2, NY // 2, 128, 12)
     mask2 = masker(24, 128, 10, 2, NX // 4, NY // 4, 64, 22)
 
-    def spread2(mine, got, rows, cells, offs):
-        rows[0, 20:24] = jnp.zeros((4, 128), F32)
-        rows[1, 20:24] = jnp.zeros((4, 128), F32)
+    def gather2(mine, got, rows, offs):
+        rows[...] = jnp.zeros((24, 128), F32)
+        rows[2 * R5 : 2 * R5 + 2] = mine[...]
+        for k in offs:
+            rows[2 * (k + R5) : 2 * (k + R5) + 2] = got[k + R5]
+
+    def unpack2(mine, got, cells, offs, scale):
         for k in [0] + offs:
-            g = mine[...] if k == 0 else got[k + R5]
-            for x in (0, 1):
-                rows[x, 2 * (k + R5) : 2 * (k + R5) + 2] = g[2 * x : 2 * x + 2]
-        cells[10] = rows[0]
-        cells[11] = rows[1]
+            v = mine[...] if k == 0 else got[k + R5]
+            i = 2 * (k + R5)
+            cells[i] = v * scale(i)
+            cells[i + 1] = pltpu.roll(v, 64, 1) * scale(i + 1)
 
     for w in wait_c2:
         w.wait_recv()
-    spread2(sc2, gc2, ac2, l2[0], offs5)
-    wait_c2 = [send(ac2, l2[0].at[2 * (R5 - k) : 2 * (R5 - k) + 2], k, 0) for k in offs5]
+    for b in (10, -10):
+        pl.semaphore_signal(far, inc=1, device_id=dev(0, b), device_id_type=MESH)
+    gather2(sc2, gc2, ac2, offs5)
+    wait_c2 = [send(ac2, rc2.at[R5 - k], k, 0) for k in offs5]
 
     for w in wait_a:
         w.wait_recv()
@@ -306,35 +315,87 @@
     lev1.build(mask1, 1, 11)
     for w in wait_c2:
         w.wait_recv()
-    for i in range(22):
-        l2[0][i] = l2[0][i] * mask2(i)
+    unpack2(ac2, rc2, l2[0], offs5, mask2)
     lev2 = Level(l2, 22, 24, 128, False)
     lev2.build(mask2, 2, 20)
+
+    def rhs(lev, f, v, i):
+        return -lev.apply(v, i) if f is None else f[i] - lev.apply(v, i)
+
+    def post(lev, f, v, w, lo, hi, out=None):
+        for i in range(lo, hi):
+            w[i] = v[i] + rhs(lev, f, v, i) * lev.iv[i] * inv_mid
+        for i in range(lo + 1, hi - 1):
+            d = w[i] - v[i]
+            e = w[i] + (keep * d + push * (rhs(lev, f, w, i) * lev.iv[i]))
+            if out is None:
+                v[i] = e
+            else:
+                out[i - lo - 1] = e[4:12]
+
+    mid2, pairs2 = chebyshev(COARSE_LOW, COARSE_HIGH, COARSE_STEPS)
+    row = iota((24, 128), 0)
+    own = jnp.where((row == 10) | (row == 11), 1.0, 0.0).astype(F32)
+    for i in range(3, 19):
+        v2a[i] = mask2(i)
+    y1[...] = dot(dot(lp1[...], v2a[7:15].reshape(192, 128)), pz1[...]).reshape(12, 16, 128)
+    den = jnp.zeros((24, 128), F32)
+    va, vb = v2a, v2b
+    for m, (k2, p2) in enumerate([(0.0, mid2)] + pairs2):
+        for i in range(4 + m, 18 - m):
+            r = lev2.apply(va, i)
+            if m == 0 and i in (10, 11):
+                den = den + own * mask2(i) * r
+            d = -p2 * (r * lev2.iv[i])
+            if m:
+                d = k2 * d2[i] + d
+            d2[i] = d
+            vb[i] = va[i] + d
+        va, vb = vb, va
+    r, c = iota((128, 96), 0), iota((128, 96), 1)
+    ci = (c * 2731) >> 16
+    spread = ((((r >> 4) - 2) >> 1) == ci - 1) & ((((r & 15) - 4) >> 1) == c - ci * 24 - 10)
+    spread = jnp.where(spread, 0.5, 0.0).astype(F32)
+    r, c = iota((128, 128), 0), iota((128, 128), 1)
+    hw[2:10] = dot(dot(spread, va[9:13].reshape(96, 128)), jnp.where((c >> 1) == r, 1.0, 0.0).astype(F32)).reshape(8, 16, 128)
+    post(lev1, None, hw, hx, 3, 9)
+    num = jnp.zeros((4, 128), F32)
+    for p in range(4):
+        num = num + hw[4 + p, 4:8] * sf1[p]
+    sg1[0:1] = jnp.sum(num, axis=0, keepdims=True)
+    sg1[1:2] = jnp.sum(den, axis=0, keepdims=True)
+
+    def broadcast(mine, got, count, offset_of, k):
+        for n in range(1, count):
+            copy = pltpu.make_async_remote_copy(src_ref=mine, dst_ref=got.at[n - 1], send_sem=gsem.at[2 * k], recv_sem=gsem.at[2 * k + 1],
+                                                device_id=dev(*offset_of(n)), device_id_type=MESH)
+            copy.start()
+        return pltpu.make_async_remote_copy(src_ref=got, dst_ref=got, send_sem=gsem.at[2 * k], recv_sem=gsem.at[2 * k + 1],
+                                            device_id=dev(*offset_of(1)), device_id_type=MESH)
+
+    pl.semaphore_wait(far, 2)
+    all_y = broadcast(sg1, rg1, NYD, lambda n: (0, n), 0)
 
     for w in wait_f1:
         w.wait_recv()
     spread1(sf1, rf1, f1)
     first(lev1, f1, v1a, 1, 11)
     second(lev1, f1, v1a, v1b, 2, 10)
+    residual(lev1, f1, v1b, r1b, 4, 8)
+    sf2[...] = pack2(dot(dot(lr1, r1b[...].reshape(64, 128)), rz1[...]))
+    wait_f2 = [send(sf2, gf2.at[R5 - k], 0, k) for k in offs4]
     for p in range(4):
         su1[p] = v1b[4 + p, 4:8]
-    residual(lev1, f1, v1b, r1b, 4, 8)
-    sf2[...] = dot(dot(lr1, r1b[...].reshape(64, 128)), rz1[...])
-    wait_f2 = [send(sf2, gf2.at[R5 - k], 0, k) for k in offs4]
     wait_u1 = [send(su1, ru1.at[n], a, b) for n, (a, b) in enumerate(NEAR)]
 
-    for x in (0, 1):
-        af2[x, 0:2] = jnp.zeros((2, 128), F32)
-        af2[x, 20:24] = jnp.zeros((4, 128), F32)
+    post(lev1, None, y1, v1a, 1, 11)
+    y0[2:14] = dot(dot(lp0[...], y1[2:10].reshape(128, 128)), pz0[...]).reshape(12, 16, 256)
+    post(lev0, None, y0, v0a, 3, 13, yout)
+
     for w in wait_f2:
         w.wait_recv()
-    for k in [0] + offs4:
-        g = sf2[...] if k == 0 else gf2[k + R5]
-        for x in (0, 1):
-            af2[x, 2 * (k + R5) : 2 * (k + R5) + 2] = g[2 * x : 2 * x + 2]
-    f2[10] = af2[0]
-    f2[11] = af2[1]
-    wait_f2 = [send(af2, f2.at[2 * (R5 - k) : 2 * (R5 - k) + 2], k, 0) for k in offs4]
+    gather2(sf2, gf2, af2, offs4)
+    wait_f2 = [send(af2, rf2.at[R5 - k], k, 0) for k in offs4]
 
     for w in wait_u1:
         w.wait_recv()
@@ -342,9 +403,13 @@
     for i in range(12):
         u1[i] = u1[i] * mask1(i)
 
+    all_y.wait_recv()
+    sg2[...] = sg1[...] + jnp.sum(rg1[...], axis=0)
+    all_x = broadcast(sg2, rg2, NXD, lambda n: (n, 0), 1)
+
     for w in wait_f2:
         w.wait_recv()
-    mid2, pairs2 = chebyshev(COARSE_LOW, COARSE_HIGH, COARSE_STEPS)
+    unpack2(af2, rf2, f2, offs4, mask2)
     for i in range(2, 20):
         d = f2[i] * lev2.iv[i] * mid2
         v2a[i] = d
@@ -358,50 +423,6 @@
             vb[i] = va[i] + d
         va, vb = vb, va
 
-    num = jnp.zeros((24, 128), F32)
-    den = jnp.zeros((24, 128), F32)
-    row = iota((24, 128), 0)
-    own = jnp.where((row == 10) | (row == 11), mask2(10), 0.0)
-    for i in range(9, 13):
-        vb[i] = mask2(i)
-    for i in (10, 11):
-        num = num + own * (f2[i] - lev2.apply(va, i))
-        den = den + own * lev2.apply(vb, i)
-    sg1[0:1] = jnp.sum(num, axis=0, keepdims=True)
-    sg1[1:2] = jnp.sum(den, axis=0, keepdims=True)
-
-    def broadcast(mine, got, count, offset_of, k):
-        copies = []
-        for n in range(1, count):
-            copy = pltpu.make_async_remote_copy(src_ref=mine, dst_ref=got.at[n - 1], send_sem=gsem.at[2 * k], recv_sem=gsem.at[2 * k + 1],
-                                                device_id=dev(*offset_of(n)), device_id_type=MESH)
-            copy.start()
-        whole = pltpu.make_async_remote_copy(src_ref=got, dst_ref=got, send_sem=gsem.at[2 * k], recv_sem=gsem.at[2 * k + 1],
-                                             device_id=dev(*offset_of(1)), device_id_type=MESH)
-        whole.wait_recv()
-        whole.wait_send()
-        return mine[...] + jnp.sum(got[...], axis=0)
-
-    sg2[...] = broadcast(sg1, rg1, NYD, lambda n: (0, n), 0)
-    total = broadcast(sg2, rg2, NXD, lambda n: (n, 0), 1)
-    num = jnp.sum(total[0:1], axis=1, keepdims=True)
-    den = jnp.sum(total[1:2], axis=1, keepdims=True)
-    shift = num / den
-    for i in range(7, 15):
-        va[i] = va[i] + shift * mask2(i)
-
-    def post(lev, f, v, w, lo, hi, out=None):
-        for i in range(lo, hi):
-            w[i] = v[i] + (f[i] - lev.apply(v, i)) * lev.iv[i] * inv_mid
-        for i in range(lo + 1, hi - 1):
-            d = w[i] - v[i]
-            r = f[i] - lev.apply(w, i)
-            e = w[i] + (keep * d + push * (r * lev.iv[i]))
-            if out is None:
-                v[i] = e
-            else:
-                out[i - lo - 1] = e[4:12]
-
     p1 = dot(dot(lp1[...], va[7:15].reshape(192, 128)), pz1[...]).reshape(12, 16, 128)
     for i in range(12):
         u1[i] = u1[i] + p1[i]
@@ -411,6 +432,14 @@
         v0b[i + 2] = v0b[i + 2] + p0[i]
     post(lev0, f0, v0b, v0a, 3, 13, o_ref)
 
+    all_x.wait_recv()
+    total = sg2[...] + jnp.sum(rg2[...], axis=0)
+    shift = jnp.sum(total[0:1], axis=1, keepdims=True) / jnp.sum(total[1:2], axis=1, keepdims=True)
+    for p in range(8):
+        o_ref[p] = o_ref[p] + shift * yout[p]
+    all_y.wait_send()
+    all_x.wait_send()
+
     for w in sends:
         w.wait_send()
 
@@ -428,11 +457,12 @@
         vm(16, 16, 256), vm(16, 16, 256), vm(16, 16, 256), level(16, 16, 256),
         vm(4, 4, 128), vm(8, 4, 4, 128), vm(4, 4, 128), vm(8, 4, 4, 128), vm(4, 4, 128), vm(8, 4, 4, 128),
         vm(12, 16, 128), vm(12, 16, 128), vm(12, 16, 128), vm(12, 16, 128), level(12, 16, 128),
-        vm(4, 128), vm(11, 4, 128), vm(2, 24, 128), vm(4, 128), vm(11, 4, 128), vm(2, 24, 128),
+        vm(2, 128), vm(11, 2, 128), vm(24, 128), vm(11, 24, 128), vm(2, 128), vm(11, 2, 128), vm(24, 128), vm(11, 24, 128),
         vm(22, 24, 128), vm(22, 24, 128), vm(22, 24, 128), vm(22, 24, 128), level(22, 24, 128),
         vm(8, 16, 256), vm(4, 16, 128), vm(192, 192), vm(192, 128), vm(256, 128), vm(128, 128), vm(128, 128), vm(128, 256),
+        vm(12, 16, 128), vm(12, 16, 128), vm(12, 16, 128), vm(16, 16, 256), vm(8, 8, 256),
         vm(2, 128), vm(NYD - 1, 2, 128), vm(2, 128), vm(NXD - 1, 2, 128),
-        pltpu.SemaphoreType.DMA((nsend,)), pltpu.SemaphoreType.DMA((nsend,)), pltpu.SemaphoreType.DMA((4,)),
+        pltpu.SemaphoreType.DMA((nsend,)), pltpu.SemaphoreType.DMA((nsend,)), pltpu.SemaphoreType.DMA((4,)), pltpu.SemaphoreType.REGULAR,
     ]
 
     def body(right_side, coefficient):

time: 56.9 us -> 41.8 us (0.73)
  Pallas kernels: 55.3 us -> 40.1 us
    pallas_call x1, Pallas kernels: 55.3 us -> 40.1 us  [body(): pl.pallas_call(body_kernel, out_shape=jax.ShapeDtypeStruct((8, 8, 256), F...]
where the time goes in v2:
time: 41.8 us; the launch traced here: 41.6 us
  Pallas kernels  40.1 us (96%)
  local copies, waits for them, and re-layouts  1.47 us (4%)
    pallas_call x1, Pallas kernels, body(): pl.pallas_call(body_kernel, out_shape=jax.ShapeDtypeStruct((8, 8, 256), F...  40.1 us
    unnamed x1, local copies, waits for them, and re-layouts  1.47 us

profile of v2, /device:TPU:1, one launch (start us, length us, event | category | flops | bytes accessed | tf_op | source)
XLA Modules:
  0.0 41.6 jit_solution(12400695912722021826)
XLA Ops:
  0.0 40.1 %shard_map.28 = f32[8,8,256]{2,1,0:T(8,128)} custom-call(f32[8,8,256]{2,1,0:T(8,128)} %f_ref.1, f32[8,8,256]{2,1,0:T(8,128)} %c_ref.1), custom_call_target="tpu_custom_call" | custom-call | tf_op jit(solution)/shard_map/pallas_call | solution.py:469
  40.1 1.5 %copy.4 = f32[8,8,256]{2,1,0:T(8,128)} copy(f32[8,8,256]{2,1,0:T(8,128)} %shard_map.28) | data formatting | bytes 131072

commit v3 on v2

--- a/solution.py
+++ b/solution.py
@@ -14,8 +14,8 @@
 F32 = jnp.float32
 NXD, NYD = 16, 32
 NX, NY, NZ = 128, 256, 256
-R5 = 5
-R4 = 4
+R2 = 4
+H2 = 2 * R2
 MESH = pl.DeviceIdType.MESH
 NEAR = [(a, b) for a in (-1, 0, 1) for b in (-1, 0, 1) if (a, b) != (0, 0)]
 
@@ -96,7 +96,7 @@
                 self.wy[i] = wyp
                 self.wz[i] = wz
                 self.dg[i] = diag
-                self.iv[i] = m / jnp.where(m > 0.5, diag, 1.0)
+                self.iv[i] = m / jnp.where(diag > 0.0, diag, 1.0)
             c = nxt
 
     def apply(self, v, i):
@@ -109,8 +109,8 @@
         return self.dg[i] * x - s
 
 
-def body_kernel(f_ref, c_ref, o_ref,
-                sy, rxf, rxc, ry, rcf, rcc, f0, v0a, v0b, l0,
+def body_kernel(f_hbm, c_hbm, o_ref,
+                f_ref, c_ref, sy, sc, rxf, rxc, ry, rc, sux, suy, rux, ruy, ruc, f0, v0a, v0b, l0,
                 sc1, rc1, sf1, rf1, su1, ru1, f1, u1, v1a, v1b, l1,
                 sc2, gc2, ac2, rc2, sf2, gf2, af2, rf2, f2, v2a, v2b, d2, l2,
                 r0b, r1b, lp1, lp0, rz0, rz1, pz1, pz0, hw, hx, y1, y0, yout,
@@ -121,11 +121,15 @@
         return (lax.rem(mx + (a + NXD), NXD), lax.rem(my + (b + NYD), NYD))
 
     partners = [(a, b) for a, b in NEAR if a and b]
-    partners += [(0, b) for b in range(-R5, R5 + 1) if b] + [(a, 0) for a in range(-R5, R5 + 1) if a]
+    partners += [(0, b) for b in range(-R2, R2 + 1) if b] + [(a, 0) for a in range(-R2, R2 + 1) if a]
     barrier = pltpu.get_barrier_semaphore()
     for a, b in partners:
         pl.semaphore_signal(barrier, inc=1, device_id=dev(a, b), device_id_type=MESH)
 
+    get_c = pltpu.make_async_copy(c_hbm, c_ref, gsem.at[4])
+    get_f = pltpu.make_async_copy(f_hbm, f_ref, gsem.at[5])
+    get_c.start()
+    get_f.start()
     sends = []
 
     def send(src, dst, a, b):
@@ -143,29 +147,34 @@
     rz1[...] = pair_sum(128, 128)
     o, q = iota((16, 64), 0), iota((16, 64), 1)
     lc1 = jnp.where(((q >> 4) == (o >> 2)) & (((q & 7) >> 1) == (o & 3)), 0.125, 0.0).astype(F32)
+    get_c.wait()
     c1own = dot(dot(lc1, c_ref[...].reshape(64, 256)), rz0[...])
     o, q = iota((4, 16), 0), iota((4, 16), 1)
     lc2 = jnp.where(((q >> 3) == (o >> 1)) & (((q & 3) >> 1) == (o & 1)), 0.125, 0.0).astype(F32)
     sc2[...] = pack2(dot(dot(lc2, c1own), rz1[...]))
     sc1[...] = c1own.reshape(4, 4, 128)
+    get_f.wait()
     for p in range(8):
         fp, cp = f_ref[p], c_ref[p]
         for s in (0, 1):
             sy[s, 0, p] = fp[4 * s : 4 * s + 4]
             sy[s, 1, p] = cp[4 * s : 4 * s + 4]
+    for sx in (0, 1):
+        for s in (0, 1):
+            sc[sx, s, 0] = c_ref[6 * sx, 6 * s : 6 * s + 2]
+            sc[sx, s, 1] = c_ref[6 * sx + 1, 6 * s : 6 * s + 2]
+            sc[sx, s, 2] = f_ref[7 * sx, 6 * s : 6 * s + 2]
     pl.semaphore_wait(barrier, len(partners))
 
-    offs5 = [k for k in range(-R5, R5 + 1) if k]
-    offs4 = [k for k in range(-R4, R4 + 1) if k]
-    wait_c2 = [send(sc2, gc2.at[R5 - k], 0, k) for k in offs5]
+    offs = [k for k in range(-R2, R2 + 1) if k]
+    wait_c2 = [send(sc2, gc2.at[R2 - k], 0, k) for k in offs]
     wait_a = []
     for sx, a in ((1, 1), (0, -1)):
         for s, b in ((1, 1), (0, -1)):
-            wait_a.append(send(sy.at[s, 1, 5:8] if sx else sy.at[s, 1, 0:3], rcc.at[1 - sx, 1 - s], a, b))
-            wait_a.append(send(sy.at[s, 0, 6:8] if sx else sy.at[s, 0, 0:2], rcf.at[1 - sx, 1 - s], a, b))
+            wait_a.append(send(sc.at[sx, s], rc.at[1 - sx, 1 - s], a, b))
     for s, a in ((1, 1), (0, -1)):
-        wait_a.append(send(c_ref.at[4:8] if s else c_ref.at[0:4], rxc.at[1 - s], a, 0))
-        wait_a.append(send(f_ref.at[5:8] if s else f_ref.at[0:3], rxf.at[1 - s], a, 0))
+        wait_a.append(send(c_ref.at[5:8] if s else c_ref.at[0:3], rxc.at[1 - s], a, 0))
+        wait_a.append(send(f_ref.at[6:8] if s else f_ref.at[0:2], rxf.at[1 - s], a, 0))
     for s, b in ((1, 1), (0, -1)):
         wait_a.append(send(sy.at[s], ry.at[1 - s], 0, b))
     wait_c1 = [send(sc1, rc1.at[n], a, b) for n, (a, b) in enumerate(NEAR)]
@@ -196,7 +205,7 @@
         ok = (gx_ >= 0) & (gx_ < nx) & (gy_ >= 0) & (gy_ < ny)
         return jnp.where(ok, w, 0.0)
 
-    lp1[...] = prolong_matrix(12, -4, -3, 24, 8, -4, -10, 4, 4, 64, 128)
+    lp1[...] = prolong_matrix(12, -4, -3, 24, 8, -4, -H2, 4, 4, 64, 128)
     lp0[...] = prolong_matrix(12, -2, -2, 16, 8, -4, -4, 8, 8, 128, 256)
     r, c = iota((128, 128), 0), iota((128, 128), 1)
     pz1[...] = jnp.where(r < 64, interp(c, r), 0.0)
@@ -219,27 +228,46 @@
 
     mask0 = masker(16, 256, 4, 8, NX, NY, 256, 16)
     mask1 = masker(16, 128, 4, 4, NX // 2, NY // 2, 128, 12)
-    mask2 = masker(24, 128, 10, 2, NX // 4, NY // 4, 64, 22)
-
-    def gather2(mine, got, rows, offs):
+    mask2 = masker(24, 128, H2, 2, NX // 4, NY // 4, 64, 2 * H2 + 2)
+
+    def gather2(mine, got, rows):
         rows[...] = jnp.zeros((24, 128), F32)
-        rows[2 * R5 : 2 * R5 + 2] = mine[...]
+        rows[H2 : H2 + 2] = mine[...]
         for k in offs:
-            rows[2 * (k + R5) : 2 * (k + R5) + 2] = got[k + R5]
-
-    def unpack2(mine, got, cells, offs, scale):
+            rows[2 * (k + R2) : 2 * (k + R2) + 2] = got[k + R2]
+
+    def unpack2(mine, got, cells):
         for k in [0] + offs:
-            v = mine[...] if k == 0 else got[k + R5]
-            i = 2 * (k + R5)
-            cells[i] = v * scale(i)
-            cells[i + 1] = pltpu.roll(v, 64, 1) * scale(i + 1)
+            v = mine[...] if k == 0 else got[k + R2]
+            i = 2 * (k + R2)
+            cells[i] = v * mask2(i)
+            cells[i + 1] = pltpu.roll(v, 64, 1) * mask2(i + 1)
+
+    def spread1(mine, got, cells):
+        for n, (a, b) in enumerate([(0, 0)] + NEAR):
+            for p in range(4):
+                x, y = 4 - 4 * a + p, 4 - 4 * b
+                cells[x, y : y + 4] = mine[p] if n == 0 else got[n - 1, p]
 
     for w in wait_c2:
         w.wait_recv()
-    for b in (10, -10):
+    for b in (8, -8):
         pl.semaphore_signal(far, inc=1, device_id=dev(0, b), device_id_type=MESH)
-    gather2(sc2, gc2, ac2, offs5)
-    wait_c2 = [send(ac2, rc2.at[R5 - k], k, 0) for k in offs5]
+    gather2(sc2, gc2, ac2)
+    wait_c2 = [send(ac2, rc2.at[R2 - k], k, 0) for k in offs]
+
+    zed1 = jnp.zeros((4, 128), F32)
+    for i in range(12):
+        l1[0][i, 12:16] = zed1
+        f1[i, 12:16] = zed1
+        u1[i, 12:16] = zed1
+    for w in wait_c1:
+        w.wait_recv()
+    spread1(sc1, rc1, l1[0])
+    for i in range(12):
+        l1[0][i] = l1[0][i] * mask1(i)
+    lev1 = Level(l1, 12, 16, 128, True)
+    lev1.build(mask1, 1, 11)
 
     for w in wait_a:
         w.wait_recv()
@@ -252,23 +280,22 @@
         c0[i, 0:4] = ry[0, 1, p]
         c0[i, 4:12] = c_ref[p]
         c0[i, 12:16] = ry[1, 1, p]
-    for p in range(4):
-        c0[p, 4:12] = rxc[0, p]
+    for p in range(3):
+        c0[1 + p, 4:12] = rxc[0, p]
         c0[12 + p, 4:12] = rxc[1, p]
-    for p in range(3):
-        f0[1 + p, 4:12] = rxf[0, p]
+    for p in range(2):
+        f0[2 + p, 4:12] = rxf[0, p]
         f0[12 + p, 4:12] = rxf[1, p]
         for s in (0, 1):
-            c0[1 + p, 12 * s : 12 * s + 4] = rcc[0, s, p]
-            c0[12 + p, 12 * s : 12 * s + 4] = rcc[1, s, p]
-    for p in range(2):
-        for s in (0, 1):
-            f0[2 + p, 12 * s : 12 * s + 4] = rcf[0, s, p]
-            f0[12 + p, 12 * s : 12 * s + 4] = rcf[1, s, p]
+            c0[2 + p, 2 + 10 * s : 4 + 10 * s] = rc[0, s, p]
+            c0[12 + p, 2 + 10 * s : 4 + 10 * s] = rc[1, s, p]
+    for s in (0, 1):
+        f0[3, 2 + 10 * s : 4 + 10 * s] = rc[0, s, 2]
+        f0[12, 2 + 10 * s : 4 + 10 * s] = rc[1, s, 2]
     for i in range(16):
         c0[i] = c0[i] * mask0(i)
     lev0 = Level(l0, 16, 16, 256, True)
-    lev0.build(mask0, 1, 15)
+    lev0.build(mask0, 2, 14)
 
     inv_mid, ((keep, push),) = chebyshev(SMOOTH_LOW, SMOOTH_HIGH, 2)
 
@@ -286,38 +313,31 @@
         for i in range(lo, hi):
             out[i - lo] = f[i] - lev.apply(v, i)
 
-    v0a[0] = zed
-    v0a[15] = zed
-    first(lev0, f0, v0a, 1, 15)
-    second(lev0, f0, v0a, v0b, 2, 14)
+    first(lev0, f0, v0a, 2, 14)
+    second(lev0, f0, v0a, v0b, 3, 13)
     residual(lev0, f0, v0b, r0b, 4, 12)
     f1own = dot(dot(lr0, r0b[...].reshape(128, 256)), rz0[...])
     sf1[...] = f1own.reshape(4, 4, 128)
     wait_f1 = [send(sf1, rf1.at[n], a, b) for n, (a, b) in enumerate(NEAR)]
 
-    def spread1(mine, got, cells):
-        for n, (a, b) in enumerate([(0, 0)] + NEAR):
-            for p in range(4):
-                x, y = 4 - 4 * a + p, 4 - 4 * b
-                cells[x, y : y + 4] = mine[p] if n == 0 else got[n - 1, p]
-
-    zed1 = jnp.zeros((4, 128), F32)
-    for i in range(12):
-        l1[0][i, 12:16] = zed1
-        f1[i, 12:16] = zed1
-        u1[i, 12:16] = zed1
-    for w in wait_c1:
-        w.wait_recv()
-    spread1(sc1, rc1, l1[0])
-    for i in range(12):
-        l1[0][i] = l1[0][i] * mask1(i)
-    lev1 = Level(l1, 12, 16, 128, True)
-    lev1.build(mask1, 1, 11)
+    for p in range(8):
+        for s in (0, 1):
+            suy[s, p] = v0b[4 + p, 4 + 6 * s : 6 + 6 * s]
+    for p in range(2):
+        for s in (0, 1):
+            sux[s, p] = v0b[4 + 6 * s + p, 4:12]
+    wait_u0 = []
+    for sx, a in ((1, 1), (0, -1)):
+        for s, b in ((1, 1), (0, -1)):
+            wait_u0.append(send(suy.at[s, 7 * sx], ruc.at[1 - sx, 1 - s], a, b))
+    wait_u0 += [send(sux.at[s], rux.at[1 - s], a, 0) for s, a in ((1, 1), (0, -1))]
+    wait_u0 += [send(suy.at[s], ruy.at[1 - s], 0, b) for s, b in ((1, 1), (0, -1))]
+
     for w in wait_c2:
         w.wait_recv()
-    unpack2(ac2, rc2, l2[0], offs5, mask2)
-    lev2 = Level(l2, 22, 24, 128, False)
-    lev2.build(mask2, 2, 20)
+    unpack2(ac2, rc2, l2[0])
+    lev2 = Level(l2, 18, 24, 128, False)
+    lev2.build(mask2, 1, 17)
 
     def rhs(lev, f, v, i):
         return -lev.apply(v, i) if f is None else f[i] - lev.apply(v, i)
@@ -335,16 +355,16 @@
 
     mid2, pairs2 = chebyshev(COARSE_LOW, COARSE_HIGH, COARSE_STEPS)
     row = iota((24, 128), 0)
-    own = jnp.where((row == 10) | (row == 11), 1.0, 0.0).astype(F32)
-    for i in range(3, 19):
+    own = jnp.where((row == H2) | (row == H2 + 1), 1.0, 0.0).astype(F32)
+    for i in range(1, 17):
         v2a[i] = mask2(i)
-    y1[...] = dot(dot(lp1[...], v2a[7:15].reshape(192, 128)), pz1[...]).reshape(12, 16, 128)
+    y1[...] = dot(dot(lp1[...], v2a[5:13].reshape(192, 128)), pz1[...]).reshape(12, 16, 128)
     den = jnp.zeros((24, 128), F32)
     va, vb = v2a, v2b
     for m, (k2, p2) in enumerate([(0.0, mid2)] + pairs2):
-        for i in range(4 + m, 18 - m):
+        for i in range(2 + m, 16 - m):
             r = lev2.apply(va, i)
-            if m == 0 and i in (10, 11):
+            if m == 0 and i in (H2, H2 + 1):
                 den = den + own * mask2(i) * r
             d = -p2 * (r * lev2.iv[i])
             if m:
@@ -354,10 +374,10 @@
         va, vb = vb, va
     r, c = iota((128, 96), 0), iota((128, 96), 1)
     ci = (c * 2731) >> 16
-    spread = ((((r >> 4) - 2) >> 1) == ci - 1) & ((((r & 15) - 4) >> 1) == c - ci * 24 - 10)
+    spread = ((((r >> 4) - 2) >> 1) == ci - 1) & ((((r & 15) - 4) >> 1) == c - ci * 24 - H2)
     spread = jnp.where(spread, 0.5, 0.0).astype(F32)
     r, c = iota((128, 128), 0), iota((128, 128), 1)
-    hw[2:10] = dot(dot(spread, va[9:13].reshape(96, 128)), jnp.where((c >> 1) == r, 1.0, 0.0).astype(F32)).reshape(8, 16, 128)
+    hw[2:10] = dot(dot(spread, va[7:11].reshape(96, 128)), jnp.where((c >> 1) == r, 1.0, 0.0).astype(F32)).reshape(8, 16, 128)
     post(lev1, None, hw, hx, 3, 9)
     num = jnp.zeros((4, 128), F32)
     for p in range(4):
@@ -382,8 +402,11 @@
     first(lev1, f1, v1a, 1, 11)
     second(lev1, f1, v1a, v1b, 2, 10)
     residual(lev1, f1, v1b, r1b, 4, 8)
-    sf2[...] = pack2(dot(dot(lr1, r1b[...].reshape(64, 128)), rz1[...]))
-    wait_f2 = [send(sf2, gf2.at[R5 - k], 0, k) for k in offs4]
+    f2own = dot(dot(lr1, r1b[...].reshape(64, 128)), rz1[...])
+    g0 = f2own[0:2] * lev2.iv[H2, H2 : H2 + 2] * mid2
+    g1 = f2own[2:4] * lev2.iv[H2 + 1, H2 : H2 + 2] * mid2
+    sf2[...] = g0 + pltpu.roll(g1, 64, 1)
+    wait_f2 = [send(sf2, gf2.at[R2 - k], 0, k) for k in offs]
     for p in range(4):
         su1[p] = v1b[4 + p, 4:8]
     wait_u1 = [send(su1, ru1.at[n], a, b) for n, (a, b) in enumerate(NEAR)]
@@ -394,8 +417,8 @@
 
     for w in wait_f2:
         w.wait_recv()
-    gather2(sf2, gf2, af2, offs4)
-    wait_f2 = [send(af2, rf2.at[R5 - k], k, 0) for k in offs4]
+    gather2(sf2, gf2, af2)
+    wait_f2 = [send(af2, rf2.at[R2 - k], k, 0) for k in offs]
 
     for w in wait_u1:
         w.wait_recv()
@@ -403,27 +426,43 @@
     for i in range(12):
         u1[i] = u1[i] * mask1(i)
 
+    for w in wait_u0:
+        w.wait_recv()
+    for p in range(8):
+        v0b[4 + p, 2:4] = ruy[0, p]
+        v0b[4 + p, 12:14] = ruy[1, p]
+    for i in (2, 3, 12, 13):
+        v0b[i] = zed
+    for p in range(2):
+        v0b[2 + p, 4:12] = rux[0, p]
+        v0b[12 + p, 4:12] = rux[1, p]
+    for s in (0, 1):
+        v0b[3, 2 + 10 * s : 4 + 10 * s] = ruc[0, s]
+        v0b[12, 2 + 10 * s : 4 + 10 * s] = ruc[1, s]
+    for i in range(2, 14):
+        v0b[i] = v0b[i] * mask0(i)
+
     all_y.wait_recv()
     sg2[...] = sg1[...] + jnp.sum(rg1[...], axis=0)
     all_x = broadcast(sg2, rg2, NXD, lambda n: (n, 0), 1)
 
     for w in wait_f2:
         w.wait_recv()
-    unpack2(af2, rf2, f2, offs4, mask2)
-    for i in range(2, 20):
-        d = f2[i] * lev2.iv[i] * mid2
-        v2a[i] = d
+    unpack2(af2, rf2, v2a)
+    for i in range(1, 17):
+        d = v2a[i]
         d2[i] = d
+        f2[i] = d * (lev2.dg[i] * (1.0 / mid2))
     va, vb = v2a, v2b
     for m, (k2, p2) in enumerate(pairs2):
-        for i in range(3 + m, 19 - m):
+        for i in range(1 + m, 17 - m):
             r = f2[i] - lev2.apply(va, i)
             d = k2 * d2[i] + p2 * (r * lev2.iv[i])
             d2[i] = d
             vb[i] = va[i] + d
         va, vb = vb, va
 
-    p1 = dot(dot(lp1[...], va[7:15].reshape(192, 128)), pz1[...]).reshape(12, 16, 128)
+    p1 = dot(dot(lp1[...], va[5:13].reshape(192, 128)), pz1[...]).reshape(12, 16, 128)
     for i in range(12):
         u1[i] = u1[i] + p1[i]
     post(lev1, f1, u1, v1a, 1, 11)
@@ -451,25 +490,26 @@
     def level(*shape):
         return [vm(*shape) for _ in range(6)]
 
-    nsend = 4 + 8 + 2 + 10 + 8 + 10 + 8 + 8 + 8 + 8
+    nsend = 4 + 4 + 2 + 8 + 8 + 8 + 8 + 8 + 8 + 8 + 8
     scratch = [
-        vm(2, 2, 8, 4, 256), vm(2, 3, 8, 256), vm(2, 4, 8, 256), vm(2, 2, 8, 4, 256), vm(2, 2, 2, 4, 256), vm(2, 2, 3, 4, 256),
+        vm(8, 8, 256), vm(8, 8, 256), vm(2, 2, 8, 4, 256), vm(2, 2, 3, 2, 256), vm(2, 2, 8, 256), vm(2, 3, 8, 256), vm(2, 2, 8, 4, 256),
+        vm(2, 2, 3, 2, 256), vm(2, 2, 8, 256), vm(2, 8, 2, 256), vm(2, 2, 8, 256), vm(2, 8, 2, 256), vm(2, 2, 2, 256),
         vm(16, 16, 256), vm(16, 16, 256), vm(16, 16, 256), level(16, 16, 256),
         vm(4, 4, 128), vm(8, 4, 4, 128), vm(4, 4, 128), vm(8, 4, 4, 128), vm(4, 4, 128), vm(8, 4, 4, 128),
         vm(12, 16, 128), vm(12, 16, 128), vm(12, 16, 128), vm(12, 16, 128), level(12, 16, 128),
-        vm(2, 128), vm(11, 2, 128), vm(24, 128), vm(11, 24, 128), vm(2, 128), vm(11, 2, 128), vm(24, 128), vm(11, 24, 128),
-        vm(22, 24, 128), vm(22, 24, 128), vm(22, 24, 128), vm(22, 24, 128), level(22, 24, 128),
+        vm(2, 128), vm(9, 2, 128), vm(24, 128), vm(9, 24, 128), vm(2, 128), vm(9, 2, 128), vm(24, 128), vm(9, 24, 128),
+        vm(18, 24, 128), vm(18, 24, 128), vm(18, 24, 128), vm(18, 24, 128), level(18, 24, 128),
         vm(8, 16, 256), vm(4, 16, 128), vm(192, 192), vm(192, 128), vm(256, 128), vm(128, 128), vm(128, 128), vm(128, 256),
         vm(12, 16, 128), vm(12, 16, 128), vm(12, 16, 128), vm(16, 16, 256), vm(8, 8, 256),
         vm(2, 128), vm(NYD - 1, 2, 128), vm(2, 128), vm(NXD - 1, 2, 128),
-        pltpu.SemaphoreType.DMA((nsend,)), pltpu.SemaphoreType.DMA((nsend,)), pltpu.SemaphoreType.DMA((4,)), pltpu.SemaphoreType.REGULAR,
+        pltpu.SemaphoreType.DMA((nsend,)), pltpu.SemaphoreType.DMA((nsend,)), pltpu.SemaphoreType.DMA((6,)), pltpu.SemaphoreType.REGULAR,
     ]
 
     def body(right_side, coefficient):
         return pl.pallas_call(
             body_kernel,
             out_shape=jax.ShapeDtypeStruct((8, 8, 256), F32),
-            in_specs=[pl.BlockSpec(memory_space=pltpu.VMEM)] * 2,
+            in_specs=[pl.BlockSpec(memory_space=pl.ANY)] * 2,
             out_specs=pl.BlockSpec(memory_space=pltpu.VMEM),
             scratch_shapes=scratch,
             compiler_params=pltpu.CompilerParams(collective_id=0, has_side_effects=True),

time: 41.8 us -> 40.7 us (0.974)
  Pallas kernels: 40.1 us -> 39 us
    pallas_call x1, Pallas kernels: 40.1 us -> 39 us  [body(): pl.pallas_call(body_kernel, out_shape=jax.ShapeDtypeStruct((8, 8, 256), F...]
where the time goes in v3:
time: 40.7 us; the launch traced here: 40.5 us
  Pallas kernels  39 us (96%)
  local copies, waits for them, and re-layouts  1.47 us (4%)
    pallas_call x1, Pallas kernels, body(): pl.pallas_call(body_kernel, out_shape=jax.ShapeDtypeStruct((8, 8, 256), F...  39 us
    unnamed x1, local copies, waits for them, and re-layouts  1.47 us

profile of v3, /device:TPU:1, one launch (start us, length us, event | category | flops | bytes accessed | tf_op | source)
XLA Modules:
  0.0 40.5 jit_solution(8910527667872750699)
XLA Ops:
  0.0 39.0 %shard_map.28 = f32[8,8,256]{2,1,0:T(8,128)} custom-call(f32[8,8,256]{2,1,0:T(8,128)} %f_hbm.1, f32[8,8,256]{2,1,0:T(8,128)} %c_hbm.1), custom_call_target="tpu_custom_call" | custom-call | tf_op jit(solution)/shard_map/pallas_call | solution.py:509
  39.1 1.5 %copy.4 = f32[8,8,256]{2,1,0:T(8,128)} copy(f32[8,8,256]{2,1,0:T(8,128)} %shard_map.28) | data formatting | bytes 131072

commit v4 on v3

--- a/solution.py
+++ b/solution.py
@@ -17,7 +17,7 @@
 R2 = 4
 H2 = 2 * R2
 MESH = pl.DeviceIdType.MESH
-NEAR = [(a, b) for a in (-1, 0, 1) for b in (-1, 0, 1) if (a, b) != (0, 0)]
+NEAR = [(1, 1), (1, -1), (-1, 1), (-1, -1), (1, 0), (-1, 0), (0, 1), (0, -1)]
 
 
 def chebyshev(low_end, high_end, sweeps):
@@ -37,8 +37,23 @@
     return lax.broadcasted_iota(jnp.int32, shape, dim)
 
 
-def dot(a, b):
-    return jnp.dot(a, b, precision=lax.Precision.HIGHEST, preferred_element_type=F32)
+def thirds(x):
+    hi = x.astype(jnp.bfloat16)
+    rest = x - hi.astype(F32)
+    mid = rest.astype(jnp.bfloat16)
+    return hi, mid, (rest - mid.astype(F32)).astype(jnp.bfloat16)
+
+
+def ldot(w, x):
+    w = w.astype(jnp.bfloat16)
+    hi, mid, lo = (jnp.dot(w, t, preferred_element_type=F32) for t in thirds(x))
+    return hi + (mid + lo)
+
+
+def rdot(x, w):
+    w = w.astype(jnp.bfloat16)
+    hi, mid, lo = (jnp.dot(t, w, preferred_element_type=F32) for t in thirds(x))
+    return hi + (mid + lo)
 
 
 def up1(v):
@@ -143,16 +158,12 @@
     def pack2(v):
         return v[0:2] + pltpu.roll(v[2:4], 64, 1)
 
-    rz0[...] = pair_sum(256, 128)
-    rz1[...] = pair_sum(128, 128)
-    o, q = iota((16, 64), 0), iota((16, 64), 1)
-    lc1 = jnp.where(((q >> 4) == (o >> 2)) & (((q & 7) >> 1) == (o & 3)), 0.125, 0.0).astype(F32)
+    o, q = iota((4, 64), 0), iota((4, 64), 1)
+    lc2 = jnp.where(((q >> 5) == (o >> 1)) & (((q & 7) >> 2) == (o & 1)), 0.015625, 0.0).astype(F32)
+    o, q = iota((256, 128), 0), iota((256, 128), 1)
+    zc2 = jnp.where((o >> 2) == q, 1.0, 0.0).astype(F32)
     get_c.wait()
-    c1own = dot(dot(lc1, c_ref[...].reshape(64, 256)), rz0[...])
-    o, q = iota((4, 16), 0), iota((4, 16), 1)
-    lc2 = jnp.where(((q >> 3) == (o >> 1)) & (((q & 3) >> 1) == (o & 1)), 0.125, 0.0).astype(F32)
-    sc2[...] = pack2(dot(dot(lc2, c1own), rz1[...]))
-    sc1[...] = c1own.reshape(4, 4, 128)
+    sc2[...] = pack2(rdot(ldot(lc2, c_ref[...].reshape(64, 256)), zc2))
     get_f.wait()
     for p in range(8):
         fp, cp = f_ref[p], c_ref[p]
@@ -166,7 +177,8 @@
             sc[sx, s, 2] = f_ref[7 * sx, 6 * s : 6 * s + 2]
     pl.semaphore_wait(barrier, len(partners))
 
-    offs = [k for k in range(-R2, R2 + 1) if k]
+    offs = [4, -4, 3, -3, 2, -2, 1, -1]
+    offx = [2, -2, 3, -3, 1, -1, 4, -4]
     wait_c2 = [send(sc2, gc2.at[R2 - k], 0, k) for k in offs]
     wait_a = []
     for sx, a in ((1, 1), (0, -1)):
@@ -177,6 +189,11 @@
         wait_a.append(send(f_ref.at[6:8] if s else f_ref.at[0:2], rxf.at[1 - s], a, 0))
     for s, b in ((1, 1), (0, -1)):
         wait_a.append(send(sy.at[s], ry.at[1 - s], 0, b))
+    rz0[...] = pair_sum(256, 128)
+    rz1[...] = pair_sum(128, 128)
+    o, q = iota((16, 64), 0), iota((16, 64), 1)
+    lc1 = jnp.where(((q >> 4) == (o >> 2)) & (((q & 7) >> 1) == (o & 3)), 0.125, 0.0).astype(F32)
+    sc1[...] = rdot(ldot(lc1, c_ref[...].reshape(64, 256)), rz0[...]).reshape(4, 4, 128)
     wait_c1 = [send(sc1, rc1.at[n], a, b) for n, (a, b) in enumerate(NEAR)]
 
     zed = jnp.zeros((16, 256), F32)
@@ -254,7 +271,7 @@
     for b in (8, -8):
         pl.semaphore_signal(far, inc=1, device_id=dev(0, b), device_id_type=MESH)
     gather2(sc2, gc2, ac2)
-    wait_c2 = [send(ac2, rc2.at[R2 - k], k, 0) for k in offs]
+    wait_c2 = [send(ac2, rc2.at[R2 - k], k, 0) for k in offx]
 
     zed1 = jnp.zeros((4, 128), F32)
     for i in range(12):
@@ -316,7 +333,7 @@
     first(lev0, f0, v0a, 2, 14)
     second(lev0, f0, v0a, v0b, 3, 13)
     residual(lev0, f0, v0b, r0b, 4, 12)
-    f1own = dot(dot(lr0, r0b[...].reshape(128, 256)), rz0[...])
+    f1own = rdot(ldot(lr0, r0b[...].reshape(128, 256)), rz0[...])
     sf1[...] = f1own.reshape(4, 4, 128)
     wait_f1 = [send(sf1, rf1.at[n], a, b) for n, (a, b) in enumerate(NEAR)]
 
@@ -358,7 +375,6 @@
     own = jnp.where((row == H2) | (row == H2 + 1), 1.0, 0.0).astype(F32)
     for i in range(1, 17):
         v2a[i] = mask2(i)
-    y1[...] = dot(dot(lp1[...], v2a[5:13].reshape(192, 128)), pz1[...]).reshape(12, 16, 128)
     den = jnp.zeros((24, 128), F32)
     va, vb = v2a, v2b
     for m, (k2, p2) in enumerate([(0.0, mid2)] + pairs2):
@@ -377,7 +393,7 @@
     spread = ((((r >> 4) - 2) >> 1) == ci - 1) & ((((r & 15) - 4) >> 1) == c - ci * 24 - H2)
     spread = jnp.where(spread, 0.5, 0.0).astype(F32)
     r, c = iota((128, 128), 0), iota((128, 128), 1)
-    hw[2:10] = dot(dot(spread, va[7:11].reshape(96, 128)), jnp.where((c >> 1) == r, 1.0, 0.0).astype(F32)).reshape(8, 16, 128)
+    hw[2:10] = rdot(ldot(spread, va[7:11].reshape(96, 128)), jnp.where((c >> 1) == r, 1.0, 0.0).astype(F32)).reshape(8, 16, 128)
     post(lev1, None, hw, hx, 3, 9)
     num = jnp.zeros((4, 128), F32)
     for p in range(4):
@@ -386,7 +402,7 @@
     sg1[1:2] = jnp.sum(den, axis=0, keepdims=True)
 
     def broadcast(mine, got, count, offset_of, k):
-        for n in range(1, count):
+        for n in sorted(range(1, count), key=lambda n: abs(n - count // 2)):
             copy = pltpu.make_async_remote_copy(src_ref=mine, dst_ref=got.at[n - 1], send_sem=gsem.at[2 * k], recv_sem=gsem.at[2 * k + 1],
                                                 device_id=dev(*offset_of(n)), device_id_type=MESH)
             copy.start()
@@ -402,7 +418,7 @@
     first(lev1, f1, v1a, 1, 11)
     second(lev1, f1, v1a, v1b, 2, 10)
     residual(lev1, f1, v1b, r1b, 4, 8)
-    f2own = dot(dot(lr1, r1b[...].reshape(64, 128)), rz1[...])
+    f2own = rdot(ldot(lr1, r1b[...].reshape(64, 128)), rz1[...])
     g0 = f2own[0:2] * lev2.iv[H2, H2 : H2 + 2] * mid2
     g1 = f2own[2:4] * lev2.iv[H2 + 1, H2 : H2 + 2] * mid2
     sf2[...] = g0 + pltpu.roll(g1, 64, 1)
@@ -411,14 +427,16 @@
         su1[p] = v1b[4 + p, 4:8]
     wait_u1 = [send(su1, ru1.at[n], a, b) for n, (a, b) in enumerate(NEAR)]
 
+    ones = jnp.concatenate([mask2(i) for i in range(5, 13)], axis=0)
+    y1[...] = rdot(ldot(lp1[...], ones), pz1[...]).reshape(12, 16, 128)
     post(lev1, None, y1, v1a, 1, 11)
-    y0[2:14] = dot(dot(lp0[...], y1[2:10].reshape(128, 128)), pz0[...]).reshape(12, 16, 256)
+    y0[2:14] = rdot(ldot(lp0[...], y1[2:10].reshape(128, 128)), pz0[...]).reshape(12, 16, 256)
     post(lev0, None, y0, v0a, 3, 13, yout)
 
     for w in wait_f2:
         w.wait_recv()
     gather2(sf2, gf2, af2)
-    wait_f2 = [send(af2, rf2.at[R2 - k], k, 0) for k in offs]
+    wait_f2 = [send(af2, rf2.at[R2 - k], k, 0) for k in offx]
 
     for w in wait_u1:
         w.wait_recv()
@@ -462,11 +480,11 @@
             vb[i] = va[i] + d
         va, vb = vb, va
 
-    p1 = dot(dot(lp1[...], va[5:13].reshape(192, 128)), pz1[...]).reshape(12, 16, 128)
+    p1 = rdot(ldot(lp1[...], va[5:13].reshape(192, 128)), pz1[...]).reshape(12, 16, 128)
     for i in range(12):
         u1[i] = u1[i] + p1[i]
     post(lev1, f1, u1, v1a, 1, 11)
-    p0 = dot(dot(lp0[...], u1[2:10].reshape(128, 128)), pz0[...]).reshape(12, 16, 256)
+    p0 = rdot(ldot(lp0[...], u1[2:10].reshape(128, 128)), pz0[...]).reshape(12, 16, 256)
     for i in range(12):
         v0b[i + 2] = v0b[i + 2] + p0[i]
     post(lev0, f0, v0b, v0a, 3, 13, o_ref)

time: 40.7 us -> 39.8 us (0.978)
  Pallas kernels: 39 us -> 38.1 us
    pallas_call x1, Pallas kernels: 39 us -> 38.1 us  [body(): pl.pallas_call(body_kernel, out_shape=jax.ShapeDtypeStruct((8, 8, 256), F...]
where the time goes in v4:
time: 39.8 us; the launch traced here: 39.6 us
  Pallas kernels  38.1 us (96%)
  local copies, waits for them, and re-layouts  1.47 us (4%)
    pallas_call x1, Pallas kernels, body(): pl.pallas_call(body_kernel, out_shape=jax.ShapeDtypeStruct((8, 8, 256), F...  38.1 us
    unnamed x1, local copies, waits for them, and re-layouts  1.47 us

profile of v4, /device:TPU:1, one launch (start us, length us, event | category | flops | bytes accessed | tf_op | source)
XLA Modules:
  0.0 39.6 jit_solution(3906598003992905237)
XLA Ops:
  0.0 38.1 %shard_map.28 = f32[8,8,256]{2,1,0:T(8,128)} custom-call(f32[8,8,256]{2,1,0:T(8,128)} %f_hbm.1, f32[8,8,256]{2,1,0:T(8,128)} %c_hbm.1), custom_call_target="tpu_custom_call" | custom-call | tf_op jit(solution)/shard_map/pallas_call | solution.py:527
  38.1 1.5 %copy.4 = f32[8,8,256]{2,1,0:T(8,128)} copy(f32[8,8,256]{2,1,0:T(8,128)} %shard_map.28) | data formatting | bytes 131072

commit v5 on v4

--- a/solution.py
+++ b/solution.py
@@ -135,16 +135,16 @@
     def dev(a, b):
         return (lax.rem(mx + (a + NXD), NXD), lax.rem(my + (b + NYD), NYD))
 
+    get_c = pltpu.make_async_copy(c_hbm, c_ref, gsem.at[4])
+    get_f = pltpu.make_async_copy(f_hbm, f_ref, gsem.at[5])
+    get_c.start()
+    get_f.start()
     partners = [(a, b) for a, b in NEAR if a and b]
     partners += [(0, b) for b in range(-R2, R2 + 1) if b] + [(a, 0) for a in range(-R2, R2 + 1) if a]
     barrier = pltpu.get_barrier_semaphore()
     for a, b in partners:
         pl.semaphore_signal(barrier, inc=1, device_id=dev(a, b), device_id_type=MESH)
 
-    get_c = pltpu.make_async_copy(c_hbm, c_ref, gsem.at[4])
-    get_f = pltpu.make_async_copy(f_hbm, f_ref, gsem.at[5])
-    get_c.start()
-    get_f.start()
     sends = []
 
     def send(src, dst, a, b):
@@ -438,6 +438,10 @@
     gather2(sf2, gf2, af2)
     wait_f2 = [send(af2, rf2.at[R2 - k], k, 0) for k in offx]
 
+    all_y.wait_recv()
+    sg2[...] = sg1[...] + jnp.sum(rg1[...], axis=0)
+    all_x = broadcast(sg2, rg2, NXD, lambda n: (n, 0), 1)
+
     for w in wait_u1:
         w.wait_recv()
     spread1(su1, ru1, u1)
@@ -459,10 +463,6 @@
         v0b[12, 2 + 10 * s : 4 + 10 * s] = ruc[1, s]
     for i in range(2, 14):
         v0b[i] = v0b[i] * mask0(i)
-
-    all_y.wait_recv()
-    sg2[...] = sg1[...] + jnp.sum(rg1[...], axis=0)
-    all_x = broadcast(sg2, rg2, NXD, lambda n: (n, 0), 1)
 
     for w in wait_f2:
         w.wait_recv()

time: 39.8 us -> 39.7 us (level)
  no operation moved by 1% of the time
where the time goes in v5:
time: 39.7 us; the launch traced here: 39.5 us
  Pallas kernels  38 us (96%)
  local copies, waits for them, and re-layouts  1.47 us (4%)
    pallas_call x1, Pallas kernels, body(): pl.pallas_call(body_kernel, out_shape=jax.ShapeDtypeStruct((8, 8, 256), F...  38 us
    unnamed x1, local copies, waits for them, and re-layouts  1.47 us

profile of v5, /device:TPU:1, one launch (start us, length us, event | category | flops | bytes accessed | tf_op | source)
XLA Modules:
  0.0 39.5 jit_solution(13522542575246204182)
XLA Ops:
  0.0 38.0 %shard_map.28 = f32[8,8,256]{2,1,0:T(8,128)} custom-call(f32[8,8,256]{2,1,0:T(8,128)} %f_hbm.1, f32[8,8,256]{2,1,0:T(8,128)} %c_hbm.1), custom_call_target="tpu_custom_call" | custom-call | tf_op jit(solution)/shard_map/pallas_call | solution.py:527
  38.0 1.5 %copy.4 = f32[8,8,256]{2,1,0:T(8,128)} copy(f32[8,8,256]{2,1,0:T(8,128)} %shard_map.28) | data formatting | bytes 131072

commit v6 on v4

--- a/solution.py
+++ b/solution.py
@@ -438,6 +438,10 @@
     gather2(sf2, gf2, af2)
     wait_f2 = [send(af2, rf2.at[R2 - k], k, 0) for k in offx]
 
+    all_y.wait_recv()
+    sg2[...] = sg1[...] + jnp.sum(rg1[...], axis=0)
+    all_x = broadcast(sg2, rg2, NXD, lambda n: (n, 0), 1)
+
     for w in wait_u1:
         w.wait_recv()
     spread1(su1, ru1, u1)
@@ -459,10 +463,6 @@
         v0b[12, 2 + 10 * s : 4 + 10 * s] = ruc[1, s]
     for i in range(2, 14):
         v0b[i] = v0b[i] * mask0(i)
-
-    all_y.wait_recv()
-    sg2[...] = sg1[...] + jnp.sum(rg1[...], axis=0)
-    all_x = broadcast(sg2, rg2, NXD, lambda n: (n, 0), 1)
 
     for w in wait_f2:
         w.wait_recv()

time: 39.8 us -> 39.7 us (level)
  no operation moved by 1% of the time
where the time goes in v6:
time: 39.7 us; the launch traced here: 39.5 us
  Pallas kernels  38 us (96%)
  local copies, waits for them, and re-layouts  1.47 us (4%)
    pallas_call x1, Pallas kernels, body(): pl.pallas_call(body_kernel, out_shape=jax.ShapeDtypeStruct((8, 8, 256), F...  38 us
    unnamed x1, local copies, waits for them, and re-layouts  1.47 us

profile of v6, /device:TPU:1, one launch (start us, length us, event | category | flops | bytes accessed | tf_op | source)
XLA Modules:
  0.0 39.5 jit_solution(9877093733898235045)
XLA Ops:
  0.0 38.0 %shard_map.28 = f32[8,8,256]{2,1,0:T(8,128)} custom-call(f32[8,8,256]{2,1,0:T(8,128)} %f_hbm.1, f32[8,8,256]{2,1,0:T(8,128)} %c_hbm.1), custom_call_target="tpu_custom_call" | custom-call | tf_op jit(solution)/shard_map/pallas_call | solution.py:527
  38.0 1.5 %copy.4 = f32[8,8,256]{2,1,0:T(8,128)} copy(f32[8,8,256]{2,1,0:T(8,128)} %shard_map.28) | data formatting | bytes 131072
